TPU v7x, 512 devices: a whole 4x4x16 slice. The times are simulated.
512 devices in a mesh: mem: 64 (over z, y), lat: 8 (over x, core).
Axes of the slice: x: 4, y: 4, z: 16, core: 2. Of those that a mesh axis runs over, the one named last changes fastest.
Arguments:
- ensemble_height_winds: float32 [512, 3, 128, 1024], P('mem', None, 'lat'), may hold values from -6 to 6
- obs_count: int32 [8, 64], P('lat'), may hold values from 16 to 128, as said below
- obs_cell: int32 [8, 64, 128], P('lat'), may hold values from 0 to 255
- obs_value: float32 [8, 64, 128], P('lat'), may hold values from -6 to 6
- obs_rinv: float32 [8, 64, 128], P('lat'), may hold values from 0.5 to 8
Outputs:
- analysis: float32 [8, 64, 512, 3, 256], P('lat', 'mem')
Inputs may be any that keep to these rules, and one draw needn't show every extreme that they name: `obs_count`: each region's count is 128, 64, 32 or 16, and some region has 128.
All inputs are finite; a program needn't handle non-finite values.
Results may differ from a plain program's by a relative error of at most 0.011.
Values may be sent and summed in bfloat16 or wider, within the bound.
No kernel may reach another device: no remote copies, remote signals or barrier semaphores. Data moves between devices by JAX's collectives and lax.ppermute only.
A program may use at most 64 MiB of HBM per device.

v0:
```python
import math

import jax
import jax.numpy as jnp
from jax import lax
from jax.sharding import PartitionSpec as P

PATCH_EDGE_LEN = 16
NS_ITERS = 5


GRAVITY = 1.0
DEPTH = 1.0
CORIOLIS = 0.25
TIME_STEP = 0.5
EDGE_WEIGHT = 0.6
CORNER_WEIGHT = 0.35
NEWTON_SCALE = 16.0


def extended_2(shard, sides, width):
    for axis, dim in sides:
        size, length = (lax.axis_size(axis), shard.shape[dim])
        up = [(i, (i + 1) % size) for i in range(size - 1)]
        down = [(j, i) for i, j in up]
        last = lax.slice_in_dim(shard, length - width, length, axis=dim)
        initial = lax.slice_in_dim(shard, 0, width, axis=dim)
        before = lax.ppermute(last, axis, up)
        after = lax.ppermute(initial, axis, down)
        shard = jnp.concatenate([before, shard, after], axis=dim)
    return shard


def tendency(padded):
    height = padded[..., 0, :, :]
    east_wind = padded[..., 1, :, :]
    north_wind = padded[..., 2, :, :]

    def along_x(quantity):
        return (quantity[..., 1:-1, 2:] - quantity[..., 1:-1, :-2]) * 0.5

    def along_y(quantity):
        return (quantity[..., 2:, 1:-1] - quantity[..., :-2, 1:-1]) * 0.5

    east_mid = east_wind[..., 1:-1, 1:-1]
    north_mid = north_wind[..., 1:-1, 1:-1]
    flux_x = (DEPTH + height) * east_wind
    flux_y = (DEPTH + height) * north_wind
    rate_height = -(along_x(flux_x) + along_y(flux_y))
    rate_east = (
        -(east_mid * along_x(east_wind) + north_mid * along_y(east_wind))
        + CORIOLIS * north_mid
        - GRAVITY * along_x(height)
    )
    rate_north = (
        -(east_mid * along_x(north_wind) + north_mid * along_y(north_wind))
        - CORIOLIS * east_mid
        - GRAVITY * along_y(height)
    )
    return jnp.stack([rate_height, rate_east, rate_north], axis=-3)


def pad_columns(quantity):
    return jnp.pad(quantity, ((0, 0), (0, 0), (0, 0), (1, 1)))


def make_block(equivalents, number, measured, precision):
    ensemble = equivalents.shape[0]
    centre = jnp.mean(equivalents, axis=0)
    slot_ids = jnp.arange(equivalents.shape[1], dtype=jnp.int32)
    weight = jnp.where(slot_ids < number, jnp.sqrt(precision), 0.0)
    scaled = (weight[:, None] * (equivalents.T - centre[:, None]) / math.sqrt(ensemble - 1)).astype(
        jnp.bfloat16
    )
    misfit = weight * (measured - centre)
    summary = jnp.dot(misfit, scaled.astype(jnp.float32), precision=lax.Precision.HIGHEST)
    return jnp.concatenate([scaled, summary.astype(jnp.bfloat16)[None, :]], axis=0)


def centre_region(region):
    flat_state = region.reshape(region.shape[0], -1)
    ens_mean = jnp.mean(flat_state, axis=0)
    return (ens_mean, (flat_state - ens_mean).astype(jnp.bfloat16))


def analyse(neighbourhood, ens_mean, deviations):
    ensemble = deviations.shape[0]
    obs_slots = neighbourhood.shape[2] - 1
    locality = [
        [CORNER_WEIGHT, EDGE_WEIGHT, CORNER_WEIGHT],
        [EDGE_WEIGHT, 1.0, EDGE_WEIGHT],
        [CORNER_WEIGHT, EDGE_WEIGHT, CORNER_WEIGHT],
    ]
    gram_sum = jnp.zeros((ensemble, ensemble), jnp.float32)
    mean_drive = jnp.zeros((ensemble,), jnp.float32)
    for row_off in range(3):
        for col_off in range(3):
            factor = locality[row_off][col_off]
            scaled = neighbourhood[row_off, col_off, :obs_slots]
            gram_sum = gram_sum + factor * lax.dot_general(
                scaled, scaled, (((0,), (0,)), ((), ())), preferred_element_type=jnp.float32
            )
            mean_drive = mean_drive + factor * neighbourhood[row_off, col_off, obs_slots].astype(
                jnp.float32
            )
    identity = jnp.eye(ensemble, dtype=jnp.float32)
    root_half = ((identity + gram_sum) / NEWTON_SCALE).astype(jnp.bfloat16)
    root_inverse = identity.astype(jnp.bfloat16)
    product = root_half.astype(jnp.float32)
    for sweep in range(NS_ITERS):
        if sweep > 0:
            product = jnp.dot(root_inverse, root_half, preferred_element_type=jnp.float32)
        correction = (1.5 * identity - 0.5 * product).astype(jnp.bfloat16)
        if sweep + 1 < NS_ITERS:
            root_half = jnp.dot(root_half, correction, preferred_element_type=jnp.float32).astype(
                jnp.bfloat16
            )
        root_inverse = jnp.dot(correction, root_inverse, preferred_element_type=jnp.float32).astype(
            jnp.bfloat16
        )
    inverse_full = root_inverse.astype(jnp.float32)
    inner_step = jnp.dot(inverse_full, mean_drive, precision=lax.Precision.HIGHEST)
    mean_weights = jnp.dot(inverse_full, inner_step, precision=lax.Precision.HIGHEST) / NEWTON_SCALE
    transform = (
        mean_weights[:, None] / math.sqrt(ensemble - 1) + inverse_full / math.sqrt(NEWTON_SCALE)
    ).astype(jnp.bfloat16)
    return ens_mean + lax.dot_general(
        transform, deviations, (((0,), (0,)), ((), ())), preferred_element_type=jnp.float32
    )


def select_row(table, position):
    return lax.dynamic_index_in_dim(table, position, 0, keepdims=False)


def per_device(ensemble_height_winds, obs_count, obs_cell, obs_value, obs_rinv):
    ensemble_sequence, gridded_numbers, latitude_lines, columns = ensemble_height_winds.shape
    patch_sequence = columns // PATCH_EDGE_LEN
    region_cells = PATCH_EDGE_LEN * PATCH_EDGE_LEN
    mem_index = lax.axis_index("mem")

    def tendency_of(current):
        extended = extended_2(current, (("lat", 2),), 1)
        return tendency(pad_columns(extended))

    section_one = ensemble_height_winds + TIME_STEP * tendency_of(ensemble_height_winds)
    section_two = 0.75 * ensemble_height_winds + 0.25 * (
        section_one + TIME_STEP * tendency_of(section_one)
    )
    propagate_ahead = ensemble_height_winds / 3.0 + 2.0 / 3.0 * (
        section_two + TIME_STEP * tendency_of(section_two)
    )
    counts_row = obs_count[0]
    cells_row = obs_cell[0]
    values_row = obs_value[0]
    rinv_row = obs_rinv[0]
    arrived = lax.all_to_all(
        propagate_ahead.reshape(
            ensemble_sequence, gridded_numbers, latitude_lines, patch_sequence, PATCH_EDGE_LEN
        )
        .transpose(3, 0, 1, 2, 4)
        .reshape(
            patch_sequence, ensemble_sequence, gridded_numbers, latitude_lines * PATCH_EDGE_LEN
        ),
        "mem",
        split_axis=0,
        concat_axis=1,
        tiled=True,
    )
    ens_mean, deviations = centre_region(arrived[0])
    heights = deviations[:, :region_cells].astype(jnp.float32)
    equivalents = jnp.take(heights, select_row(cells_row, mem_index), axis=1)
    neighbourhood = extended_2(
        make_block(
            equivalents,
            select_row(counts_row, mem_index),
            select_row(values_row, mem_index),
            select_row(rinv_row, mem_index),
        )[None, None],
        (("mem", 1), ("lat", 0)),
        1,
    )
    analysed = analyse(neighbourhood, ens_mean, deviations)
    return analysed.reshape(deviations.shape[0], gridded_numbers, region_cells)[None, None]


def solution(mesh):
    in_specs = (
        P("mem", None, "lat", None),
        P("lat", None),
        P("lat", None, None),
        P("lat", None, None),
        P("lat", None, None),
    )
    out_specs = P("lat", "mem", None, None, None)
    return jax.shard_map(
        per_device, mesh=mesh, in_specs=in_specs, out_specs=out_specs, check_vma=False
    )
```

profile of v0, /device:TPU:1, one launch (start us, length us, event | category | flops | bytes accessed | tf_op | source)
XLA Modules:
  0.0 195.6 jit_solution(2587379778674130609)
XLA Ops:
  0.0 2.3 %copy.38 = f32[8,3,16,1024]{3,0,2,1:T(8,128)S(1)} copy(f32[8,3,16,1024]{3,2,1,0:T(8,128)} %param.5) | data formatting | bytes 3145728 | tf_op args[0]
  2.4 4.5 %collective-permute-start = (f32[8,3,1,1024]{3,0,2,1:T(8,128)S(1)}, f32[8,3,1,1024]{3,0,2,1:T(8,128)S(1)}, u32[]{:S(2)}, u32[]{:S(2)}) collective-permute-start(f32[8,3,1,1024]{3,0,2,1:T(8,128)S(1)} %get-tuple-element.30), channel_id=1, source_target_pairs={{0,1},{1,2},{2,3},{3,4},{4,5},{5,6},{6,7},{8,9},{9,10},{10,11},{11... | collective-permute-start | bytes 294920 | tf_op jit(solution)/shard_map/ppermute | solution.py:28
  6.9 5.5 %collective-permute-start.1 = (f32[8,3,1,1024]{3,0,2,1:T(8,128)S(1)}, f32[8,3,1,1024]{3,0,2,1:T(8,128)S(1)}, u32[]{:S(2)}, u32[]{:S(2)}) collective-permute-start(f32[8,3,1,1024]{3,0,2,1:T(8,128)S(1)} %get-tuple-element.31), channel_id=1, source_target_pairs={{1,0},{2,1},{3,2},{4,3},{5,4},{6,5},{7,6},{9,8},{10,9},{11,10},{12... | collective-permute-start | bytes 294920 | tf_op jit(solution)/shard_map/ppermute | solution.py:29
  14.7 1.6 fusion.85
  17.4 1.9 collective-permute-start.2
  19.4 2.4 %collective-permute-start.3 = (f32[8,3,1,1024]{3,0,2,1:T(8,128)S(1)}, f32[8,3,1,1024]{3,0,2,1:T(8,128)S(1)}, u32[]{:S(2)}, u32[]{:S(2)}) collective-permute-start(f32[8,3,1,1024]{3,0,2,1:T(8,128)S(1)} %get-tuple-element.29), channel_id=1, source_target_pairs={{1,0},{2,1},{3,2},{4,3},{5,4},{6,5},{7,6},{9,8},{10,9},{11,10},{12... | collective-permute-start | bytes 294920 | tf_op jit(solution)/shard_map/ppermute | solution.py:29
  21.8 3.5 %collective-permute-done.3 = f32[8,3,1,1024]{3,0,2,1:T(8,128)S(1)} collective-permute-done((f32[8,3,1,1024]{3,0,2,1:T(8,128)S(1)}, f32[8,3,1,1024]{3,0,2,1:T(8,128)S(1)}, u32[]{:S(2)}, u32[]{:S(2)}) %collective-permute-start.3) | collective-permute-done | bytes 98336 | tf_op jit(solution)/shard_map/ppermute | solution.py:29
  26.6 1.6 fusion.61
  29.6 1.9 collective-permute-start.4
  31.6 2.6 %collective-permute-start.5 = (f32[8,3,1,1024]{3,0,2,1:T(8,128)S(1)}, f32[8,3,1,1024]{3,0,2,1:T(8,128)S(1)}, u32[]{:S(2)}, u32[]{:S(2)}) collective-permute-start(f32[8,3,1,1024]{3,0,2,1:T(8,128)S(1)} %get-tuple-element.27), channel_id=1, source_target_pairs={{1,0},{2,1},{3,2},{4,3},{5,4},{6,5},{7,6},{9,8},{10,9},{11,10},{12... | collective-permute-start | bytes 294920 | tf_op jit(solution)/shard_map/ppermute | solution.py:29
  34.2 3.3 %collective-permute-done.5 = f32[8,3,1,1024]{3,0,2,1:T(8,128)S(1)} collective-permute-done((f32[8,3,1,1024]{3,0,2,1:T(8,128)S(1)}, f32[8,3,1,1024]{3,0,2,1:T(8,128)S(1)}, u32[]{:S(2)}, u32[]{:S(2)}) %collective-permute-start.5) | collective-permute-done | bytes 98336 | tf_op jit(solution)/shard_map/ppermute | solution.py:29
  38.8 1.6 fusion.37
  40.4 1.7 fusion.7
  43.0 7.0 %reshape.105 = f32[8,3,16,64,16]{4,3,2,1,0:T(8,128)} reshape(f32[8,3,16,1024]{3,2,1,0:T(8,128)S(1)} %copy.44) | data formatting | bytes 3145728 | tf_op jit(solution)/shard_map/reshape | solution.py:158
  50.0 7.5 %copy.45 = f32[64,8,3,16,16]{0,4,3,2,1:T(8,128)S(1)} copy(f32[64,8,3,16,16]{4,0,3,2,1:T(8,128)} %bitcast.155) | data formatting | bytes 3145728 | tf_op jit(solution)/shard_map/transpose | solution.py:161
  57.5 2.0 %copy.46 = f32[64,8,3,256]{3,1,2,0:T(8,128)} copy(f32[64,8,3,256]{0,3,2,1:T(8,128)S(1)} %bitcast.157) | data formatting | bytes 3145728 | tf_op jit(solution)/shard_map/reshape | solution.py:162
  59.5 17.9 %all-to-all-start = ((f32[64,8,3,256]{3,1,2,0:T(8,128)}), f32[64,8,3,256]{3,1,2,0:T(8,128)S(1)}, u32[]{:S(2)}, u32[]{:S(2)}) async-start(f32[64,8,3,256]{3,1,2,0:T(8,128)} %copy.46), calls=%async_computation | async-start | bytes 3145728 | tf_op jit(solution)/shard_map/all_to_all | solution.py:157
  79.4 74.5 %all-to-all-done = f32[64,8,3,256]{3,1,2,0:T(8,128)S(1)} async-done(((f32[64,8,3,256]{3,1,2,0:T(8,128)}), f32[64,8,3,256]{3,1,2,0:T(8,128)S(1)}, u32[]{:S(2)}, u32[]{:S(2)}) %all-to-all-start) | async-done | bytes 1572896 | tf_op jit(solution)/shard_map/all_to_all | solution.py:157
  158.6 3.1 %collective-permute-start.6 = (bf16[1,1,129,512]{3,2,1,0:T(8,128)(2,1)S(1)}, bf16[1,1,129,512]{3,2,1,0:T(8,128)(2,1)S(1)}, u32[]{:S(2)}, u32[]{:S(2)}) collective-permute-start(bf16[1,1,129,512]{3,2,1,0:T(8,128)(2,1)S(1)} %maximum_bitcast_fusion), channel_id=1, source_target_pairs={{0,8},{8,16},{16,24},{24,32},{32,40},{40,48},{48,56},{56,64},{64,7... | collective-permute-start | bytes 396296 | tf_op jit(solution)/shard_map/ppermute | solution.py:28
  163.7 4.0 %collective-permute-done.7 = bf16[1,1,129,512]{3,2,1,0:T(8,128)(2,1)S(1)} collective-permute-done((bf16[1,1,129,512]{3,2,1,0:T(8,128)(2,1)S(1)}, bf16[1,1,129,512]{3,2,1,0:T(8,128)(2,1)S(1)}, u32[]{:S(2)}, u32[]{:S(2)}) %collective-permute-start.7) | collective-permute-done | bytes 132128 | tf_op jit(solution)/shard_map/ppermute | solution.py:29
  167.8 6.0 %collective-permute-start.8 = (bf16[1,3,129,512]{3,2,1,0:T(8,128)(2,1)S(1)}, bf16[1,3,129,512]{3,2,1,0:T(8,128)(2,1)S(1)}, u32[]{:S(2)}, u32[]{:S(2)}) collective-permute-start(bf16[1,3,129,512]{3,2,1,0:T(8,128)(2,1)S(1)} %pad_maximum_fusion), channel_id=1, source_target_pairs={{0,1},{1,2},{2,3},{3,4},{4,5},{5,6},{6,7},{8,9},{9,10},{10,11},{11... | collective-permute-start | bytes 1188872 | tf_op jit(solution)/shard_map/ppermute | solution.py:28
  173.8 2.1 %collective-permute-start.9 = (bf16[1,3,129,512]{3,2,1,0:T(8,128)(2,1)S(1)}, bf16[1,3,129,512]{3,2,1,0:T(8,128)(2,1)S(1)}, u32[]{:S(2)}, u32[]{:S(2)}) collective-permute-start(bf16[1,3,129,512]{3,2,1,0:T(8,128)(2,1)S(1)} %pad_maximum_fusion), channel_id=1, source_target_pairs={{1,0},{2,1},{3,2},{4,3},{5,4},{6,5},{7,6},{9,8},{10,9},{11,10},{12... | collective-permute-start | bytes 1188872 | tf_op jit(solution)/shard_map/ppermute | solution.py:29
  176.6 6.6 %collective-permute-done.9 = bf16[1,3,129,512]{3,2,1,0:T(8,128)(2,1)S(1)} collective-permute-done((bf16[1,3,129,512]{3,2,1,0:T(8,128)(2,1)S(1)}, bf16[1,3,129,512]{3,2,1,0:T(8,128)(2,1)S(1)}, u32[]{:S(2)}, u32[]{:S(2)}) %collective-permute-start.9) | collective-permute-done | bytes 396320 | tf_op jit(solution)/shard_map/ppermute | solution.py:29
  194.0 1.6 copy.49
  (80 shorter events, 28.3 us)
Async XLA Ops:
  0.0 77.4 %copy-start = (s32[1,64]{1,0:T(1,128)S(1)}, s32[1,64]{1,0:T(1,128)}, u32[]{:S(2)}) copy-start(s32[1,64]{1,0:T(1,128)} %param.6) | copy-start | bytes 772
  2.4 10.1 %collective-permute-start = (f32[8,3,1,1024]{3,0,2,1:T(8,128)S(1)}, f32[8,3,1,1024]{3,0,2,1:T(8,128)S(1)}, u32[]{:S(2)}, u32[]{:S(2)}) collective-permute-start(f32[8,3,1,1024]{3,0,2,1:T(8,128)S(1)} %get-tuple-element.30), channel_id=1, source_target_pairs={{0,1},{1,2},{2,3},{3,4},{4,5},{5,6},{6,7},{8,9},{9,10},{10,11},{11... | collective-permute-start | bytes 294920 | tf_op jit(solution)/shard_map/ppermute | solution.py:28
  6.9 6.5 %collective-permute-start.1 = (f32[8,3,1,1024]{3,0,2,1:T(8,128)S(1)}, f32[8,3,1,1024]{3,0,2,1:T(8,128)S(1)}, u32[]{:S(2)}, u32[]{:S(2)}) collective-permute-start(f32[8,3,1,1024]{3,0,2,1:T(8,128)S(1)} %get-tuple-element.31), channel_id=1, source_target_pairs={{1,0},{2,1},{3,2},{4,3},{5,4},{6,5},{7,6},{9,8},{10,9},{11,10},{12... | collective-permute-start | bytes 294920 | tf_op jit(solution)/shard_map/ppermute | solution.py:29
  14.7 1.6 copy-start.1
  17.4 4.3 %collective-permute-start.2 = (f32[8,3,1,1024]{3,0,2,1:T(8,128)S(1)}, f32[8,3,1,1024]{3,0,2,1:T(8,128)S(1)}, u32[]{:S(2)}, u32[]{:S(2)}) collective-permute-start(f32[8,3,1,1024]{3,0,2,1:T(8,128)S(1)} %get-tuple-element.28), channel_id=1, source_target_pairs={{0,1},{1,2},{2,3},{3,4},{4,5},{5,6},{6,7},{8,9},{9,10},{10,11},{11... | collective-permute-start | bytes 294920 | tf_op jit(solution)/shard_map/ppermute | solution.py:28
  19.4 5.9 %collective-permute-start.3 = (f32[8,3,1,1024]{3,0,2,1:T(8,128)S(1)}, f32[8,3,1,1024]{3,0,2,1:T(8,128)S(1)}, u32[]{:S(2)}, u32[]{:S(2)}) collective-permute-start(f32[8,3,1,1024]{3,0,2,1:T(8,128)S(1)} %get-tuple-element.29), channel_id=1, source_target_pairs={{1,0},{2,1},{3,2},{4,3},{5,4},{6,5},{7,6},{9,8},{10,9},{11,10},{12... | collective-permute-start | bytes 294920 | tf_op jit(solution)/shard_map/ppermute | solution.py:29
  29.6 4.5 %collective-permute-start.4 = (f32[8,3,1,1024]{3,0,2,1:T(8,128)S(1)}, f32[8,3,1,1024]{3,0,2,1:T(8,128)S(1)}, u32[]{:S(2)}, u32[]{:S(2)}) collective-permute-start(f32[8,3,1,1024]{3,0,2,1:T(8,128)S(1)} %get-tuple-element.26), channel_id=1, source_target_pairs={{0,1},{1,2},{2,3},{3,4},{4,5},{5,6},{6,7},{8,9},{9,10},{10,11},{11... | collective-permute-start | bytes 294920 | tf_op jit(solution)/shard_map/ppermute | solution.py:28
  31.6 5.9 %collective-permute-start.5 = (f32[8,3,1,1024]{3,0,2,1:T(8,128)S(1)}, f32[8,3,1,1024]{3,0,2,1:T(8,128)S(1)}, u32[]{:S(2)}, u32[]{:S(2)}) collective-permute-start(f32[8,3,1,1024]{3,0,2,1:T(8,128)S(1)} %get-tuple-element.27), channel_id=1, source_target_pairs={{1,0},{2,1},{3,2},{4,3},{5,4},{6,5},{7,6},{9,8},{10,9},{11,10},{12... | collective-permute-start | bytes 294920 | tf_op jit(solution)/shard_map/ppermute | solution.py:29
  59.5 94.4 %all-to-all-start = ((f32[64,8,3,256]{3,1,2,0:T(8,128)}), f32[64,8,3,256]{3,1,2,0:T(8,128)S(1)}, u32[]{:S(2)}, u32[]{:S(2)}) async-start(f32[64,8,3,256]{3,1,2,0:T(8,128)} %copy.46), calls=%async_computation | async-start | bytes 3145728 | tf_op jit(solution)/shard_map/all_to_all | solution.py:157
  154.2 0.9 copy-start.2
  158.6 5.1 %collective-permute-start.6 = (bf16[1,1,129,512]{3,2,1,0:T(8,128)(2,1)S(1)}, bf16[1,1,129,512]{3,2,1,0:T(8,128)(2,1)S(1)}, u32[]{:S(2)}, u32[]{:S(2)}) collective-permute-start(bf16[1,1,129,512]{3,2,1,0:T(8,128)(2,1)S(1)} %maximum_bitcast_fusion), channel_id=1, source_target_pairs={{0,8},{8,16},{16,24},{24,32},{32,40},{40,48},{48,56},{56,64},{64,7... | collective-permute-start | bytes 396296 | tf_op jit(solution)/shard_map/ppermute | solution.py:28
  161.7 6.0 %collective-permute-start.7 = (bf16[1,1,129,512]{3,2,1,0:T(8,128)(2,1)S(1)}, bf16[1,1,129,512]{3,2,1,0:T(8,128)(2,1)S(1)}, u32[]{:S(2)}, u32[]{:S(2)}) collective-permute-start(bf16[1,1,129,512]{3,2,1,0:T(8,128)(2,1)S(1)} %maximum_bitcast_fusion), channel_id=1, source_target_pairs={{8,0},{16,8},{24,16},{32,24},{40,32},{48,40},{56,48},{64,56},{72,6... | collective-permute-start | bytes 396296 | tf_op jit(solution)/shard_map/ppermute | solution.py:29
  167.8 16.4 %collective-permute-start.8 = (bf16[1,3,129,512]{3,2,1,0:T(8,128)(2,1)S(1)}, bf16[1,3,129,512]{3,2,1,0:T(8,128)(2,1)S(1)}, u32[]{:S(2)}, u32[]{:S(2)}) collective-permute-start(bf16[1,3,129,512]{3,2,1,0:T(8,128)(2,1)S(1)} %pad_maximum_fusion), channel_id=1, source_target_pairs={{0,1},{1,2},{2,3},{3,4},{4,5},{5,6},{6,7},{8,9},{9,10},{10,11},{11... | collective-permute-start | bytes 1188872 | tf_op jit(solution)/shard_map/ppermute | solution.py:28
  173.8 9.4 %collective-permute-start.9 = (bf16[1,3,129,512]{3,2,1,0:T(8,128)(2,1)S(1)}, bf16[1,3,129,512]{3,2,1,0:T(8,128)(2,1)S(1)}, u32[]{:S(2)}, u32[]{:S(2)}) collective-permute-start(bf16[1,3,129,512]{3,2,1,0:T(8,128)(2,1)S(1)} %pad_maximum_fusion), channel_id=1, source_target_pairs={{1,0},{2,1},{3,2},{4,3},{5,4},{6,5},{7,6},{9,8},{10,9},{11,10},{12... | collective-permute-start | bytes 1188872 | tf_op jit(solution)/shard_map/ppermute | solution.py:29
  183.2 2.2 %copy-start.4 = (bf16[1,3,129,512]{3,2,1,0:T(8,128)(2,1)}, bf16[1,3,129,512]{3,2,1,0:T(8,128)(2,1)S(1)}, u32[]{:S(2)}) copy-start(bf16[1,3,129,512]{3,2,1,0:T(8,128)(2,1)S(1)} %collective-permute-done.9) | copy-start | bytes 1188868
  190.3 2.5 %copy-start.3 = (bf16[512,768]{1,0:T(8,128)(2,1)S(1)}, bf16[512,768]{1,0:T(8,128)(2,1)}, u32[]{:S(2)}) copy-start(bf16[512,768]{1,0:T(8,128)(2,1)} %copy-done.2) | copy-start | bytes 2359300
where the time goes:
time: 196 us
  waiting for transfers between devices  93.2 us (48%)
  starting transfers between devices  49.4 us (25%)
  local copies, waits for them, and re-layouts  24.7 us (13%)
  other arithmetic  15.8 us (8%)
  matrix products  12 us (6%)
    all_to_all x1, waiting for transfers between devices, per_device(): lax.all_to_all(propagate_ahead.reshape(ensemble_sequence, gridded_numbers...  74.5 us
    ppermute x5, waiting for transfers between devices, extended_2(): after = lax.ppermute(initial, axis, down)  18.3 us
    all_to_all x1, starting transfers between devices, per_device(): lax.all_to_all(propagate_ahead.reshape(ensemble_sequence, gridded_numbers...  17.9 us
    ppermute x5, starting transfers between devices, extended_2(): before = lax.ppermute(last, axis, up)  17.5 us
    ppermute x5, starting transfers between devices, extended_2(): after = lax.ppermute(initial, axis, down)  14 us
    transpose x1, local copies, waits for them, and re-layouts, per_device(): arrived = lax.all_to_all(propagate_ahead.reshape(ensemble_sequence, gridd...  7.48 us
    reshape x1, local copies, waits for them, and re-layouts, per_device(): propagate_ahead.reshape(ensemble_sequence, gridded_numbers, latitude_line...  6.96 us
    another operation x6, other arithmetic, tendency(): return jnp.stack([rate_height, rate_east, rate_north], axis=-3)  6.12 us
  transfers between devices with their start and end apart: 11, of which 7 were waited for; matrix products, arithmetic and copies ran while one was open for 2% of the time, Pallas kernels for 0%

commit v1 on v0

v1 whole, which is shorter than its diff:
```python
import math


import jax
import jax.numpy as jnp
from jax import lax
from jax.experimental import pallas as pl
from jax.experimental.pallas import tpu as pltpu
from jax.sharding import PartitionSpec as P

EDGE = 16
NS_ITERS = 5
EDGE_WEIGHT = 0.6
CORNER_WEIGHT = 0.35
NEWTON_SCALE = 16.0
HALO = 3
LANES = 128

bf16 = jnp.bfloat16
f32 = jnp.float32


def vmem_spec():
    return pl.BlockSpec(memory_space=pltpu.VMEM)


def smem_spec():
    return pl.BlockSpec(memory_space=pltpu.SMEM)


def tile_shifts(load, n, lane):
    tiles, ahead, behind = {}, {}, {}

    def get(t):
        if t not in tiles:
            tiles[t] = load(t)
            ahead[t] = pltpu.roll(tiles[t], LANES - 1, 1)
            behind[t] = pltpu.roll(tiles[t], 1, 1)

    def at(t):
        get(t)
        if t + 1 < n:
            get(t + 1)
        edge = ahead[t + 1] if t + 1 < n else jnp.zeros_like(tiles[t])
        plus = jnp.where(lane == LANES - 1, edge, ahead[t])
        edge = behind[t - 1] if t > 0 else jnp.zeros_like(tiles[t])
        minus = jnp.where(lane == 0, edge, behind[t])
        return tiles[t], plus - minus

    return at


def advance(src, i, lane, n_tiles):
    def load(f, k):
        return lambda t: src[f, k, :, t * LANES : (t + 1) * LANES]

    h_at = tile_shifts(load(0, i), n_tiles, lane)
    u_at = tile_shifts(load(1, i), n_tiles, lane)
    v_at = tile_shifts(load(2, i), n_tiles, lane)
    flux_at = tile_shifts(
        lambda t: (1.0 + load(0, i)(t)) * load(1, i)(t), n_tiles, lane
    )
    for t in range(n_tiles):
        h, dh = h_at(t)
        u, du = u_at(t)
        v, dv = v_at(t)
        _, df = flux_at(t)
        hu, hd = load(0, i + 1)(t), load(0, i - 1)(t)
        vu, vd = load(2, i + 1)(t), load(2, i - 1)(t)
        dyu = load(1, i + 1)(t) - load(1, i - 1)(t)
        dyf = (1.0 + hu) * vu - (1.0 + hd) * vd
        qu, qv = 0.25 * u, 0.25 * v
        yield t, (
            h - 0.25 * (df + dyf),
            u - (qu * du + qv * (dyu - 0.5) + 0.25 * dh),
            v - (qu * (dv + 0.5) + qv * (vu - vd) + 0.25 * (hu - hd)),
        )


def edge_kernel(x_ref, first_ref, last_ref, sems):
    rows = x_ref.shape[2]
    copies = []
    for f in range(3):
        for k in range(HALO):
            for e, (dst, r) in enumerate(((first_ref, k), (last_ref, rows - HALO + k))):
                copies.append(
                    pltpu.make_async_copy(x_ref.at[:, f, r], dst.at[f, k], sems.at[(f * HALO + k) * 2 + e])
                )
    for c in copies:
        c.start()
    for c in copies:
        c.wait()


def edge_rows(x):
    members, fields, _, columns = x.shape
    part = jax.ShapeDtypeStruct((fields, HALO, members, columns), f32)
    return pl.pallas_call(
        edge_kernel,
        out_shape=(part, part),
        in_specs=[pl.BlockSpec(memory_space=pl.ANY)],
        out_specs=(vmem_spec(), vmem_spec()),
        scratch_shapes=[pltpu.SemaphoreType.DMA((fields * HALO * 2,))],
        compiler_params=pltpu.CompilerParams(vmem_limit_bytes=4 << 20),
        name="edges",
    )(x)


def inner_kernel(x_ref, s3_ref, s1e_ref, s2e_ref, q, a, b, sems):
    rows = x_ref.shape[2]
    n_tiles = x_ref.shape[3] // LANES
    copies = [
        pltpu.make_async_copy(x_ref.at[:, f, r], q.at[f, r], sems.at[f * rows + r])
        for r in range(rows)
        for f in range(3)
    ]
    for c in copies:
        c.start()
    for c in copies:
        c.wait()
    lane = lax.broadcasted_iota(jnp.int32, (8, LANES), 1)

    def section(src, dst, lo, hi, off, combine):
        @pl.loop(lo, hi, unroll=2)
        def _(i):
            for t, new in advance(src, i, lane, n_tiles):
                sl = slice(t * LANES, (t + 1) * LANES)
                for f in range(3):
                    dst[f, i - off, :, sl] = combine(new[f], lambda: q[f, i, :, sl])

    section(q, a, 1, rows - 1, 0, lambda s, q0: s)
    section(a, b, 2, rows - 2, 0, lambda s, q0: 0.75 * q0() + 0.25 * s)
    section(b, s3_ref, 3, rows - 3, 3, lambda s, q0: q0() * (1.0 / 3.0) + (2.0 / 3.0) * s)
    s1e_ref[:, :2] = a[:, 1:3]
    s1e_ref[:, 2:] = a[:, rows - 3 : rows - 1]
    s2e_ref[:, :2] = b[:, 2:4]
    s2e_ref[:, 2:] = b[:, rows - 4 : rows - 2]


def inner_forecast(x):
    members, fields, rows, columns = x.shape

    def part(n):
        return jax.ShapeDtypeStruct((fields, n, members, columns), f32)

    return pl.pallas_call(
        inner_kernel,
        out_shape=(part(rows - 2 * HALO), part(4), part(4)),
        in_specs=[pl.BlockSpec(memory_space=pl.ANY)],
        out_specs=(vmem_spec(),) * 3,
        scratch_shapes=[pltpu.VMEM((fields, rows, members, columns), f32)] * 3
        + [pltpu.SemaphoreType.DMA((fields * rows,))],
        compiler_params=pltpu.CompilerParams(vmem_limit_bytes=12 << 20),
        cost_estimate=pl.CostEstimate(flops=4 * 10**8, bytes_accessed=4 * 10**6, transcendentals=0),
        name="inner",
    )(x)


def outer_kernel(
    row_ref, top_ref, first_ref, last_ref, bottom_ref, s1e_ref, s2e_ref, s3_ref, h_ref, uv_ref, q, a, b, c
):
    rows = s3_ref.shape[1] + 2 * HALO
    n_tiles = s3_ref.shape[3] // LANES
    lane = lax.broadcasted_iota(jnp.int32, (8, LANES), 1)
    q[:, 0:3] = top_ref[...]
    q[:, 3:6] = first_ref[...]
    q[:, 6:9] = last_ref[...]
    q[:, 9:12] = bottom_ref[...]
    a[:, 3:7] = s1e_ref[...]
    b[:, 3:7] = s2e_ref[...]

    def section(src, dst, centre_jump, dst_jump, q_at, combine):
        @pl.loop(0, 2 * HALO, unroll=6)
        def _(i):
            low = (i >= HALO).astype(jnp.int32)
            at, to, qi = i + 1 + centre_jump * low, i + dst_jump * low, q_at(i, low)
            for t, new in advance(src, at, lane, n_tiles):
                sl = slice(t * LANES, (t + 1) * LANES)
                for f in range(3):
                    dst[f, to, :, sl] = combine(new[f], lambda: q[f, qi, :, sl])

    def clear(ref, top_at, bottom_at):
        @pl.when(row_ref[0] == 0)
        def _():
            ref[:, top_at] = jnp.zeros_like(ref[:, top_at])

        @pl.when(row_ref[0] == row_ref[1] - 1)
        def _():
            ref[:, bottom_at] = jnp.zeros_like(ref[:, bottom_at])

    section(q, a, 4, 4, lambda i, low: i, lambda s, q0: s)
    clear(a, 1, 8)
    section(a, b, 2, 4, lambda i, low: i + 2 + 2 * low, lambda s, q0: 0.75 * q0() + 0.25 * s)
    clear(b, 0, 9)
    section(b, c, 2, 0, lambda i, low: i + 3, lambda s, q0: q0() * (1.0 / 3.0) + (2.0 / 3.0) * s)

    block = lane // EDGE
    keep = {bit: (block & bit) == 0 for bit in (1, 2, 4)}

    def final_row(f, r, col):
        if r < HALO:
            return c[f, r, :, col]
        if r >= rows - HALO:
            return c[f, r - rows + 2 * HALO, :, col]
        return s3_ref[f, r - HALO, :, col]

    @pl.loop(0, n_tiles)
    def _(t):
        col = pl.ds(pl.multiple_of(t * LANES, LANES), LANES)
        for f in range(3):
            for half in range(rows // 8):
                v = [final_row(f, half * 8 + r, col) for r in range(8)]
                for bit in (4, 2, 1):
                    for i in range(8):
                        if i & bit:
                            continue
                        lo, hi = v[i], v[i | bit]
                        v[i] = jnp.where(keep[bit], lo, pltpu.roll(hi, bit * EDGE, 1))
                        v[i | bit] = jnp.where(keep[bit], pltpu.roll(lo, LANES - bit * EDGE, 1), hi)
                for d in range(8):
                    if f == 0:
                        h_ref[t * 8 + d, half] = v[d].astype(bf16)
                    else:
                        uv_ref[t * 8 + d, (f - 1) * 2 + half] = v[d].astype(bf16)


def outer_forecast(row, top, first, last, bottom, s1e, s2e, s3):
    fields, _, members, columns = s3.shape
    n_dest = columns // EDGE

    def scratch(n):
        return pltpu.VMEM((fields, n, members, columns), f32)

    return pl.pallas_call(
        outer_kernel,
        out_shape=(
            jax.ShapeDtypeStruct((n_dest, 2, members, LANES), bf16),
            jax.ShapeDtypeStruct((n_dest, 4, members, LANES), bf16),
        ),
        in_specs=[smem_spec()] + [vmem_spec()] * 7,
        out_specs=(vmem_spec(), vmem_spec()),
        scratch_shapes=[scratch(12), scratch(10), scratch(10), scratch(6)],
        compiler_params=pltpu.CompilerParams(vmem_limit_bytes=16 << 20),
        cost_estimate=pl.CostEstimate(flops=2 * 10**8, bytes_accessed=4 * 10**6, transcendentals=0),
        name="outer",
    )(row, top, first, last, bottom, s1e, s2e, s3)


def split3(row):
    high = row.astype(bf16)
    rest = row - high.astype(f32)
    mid = rest.astype(bf16)
    low = (rest - mid.astype(f32)).astype(bf16)
    zero = jnp.zeros((5, row.shape[1]), f32)
    return jnp.concatenate([high.astype(f32), mid.astype(f32), low.astype(f32), zero], axis=0).astype(bf16)


def centred(slab):
    value = slab.astype(f32).reshape(-1, LANES)
    mean = jnp.sum(value, axis=0, keepdims=True) * (1.0 / value.shape[0])
    return mean, (value - mean).astype(bf16)


def block_kernel(at_ref, count_ref, cell_ref, value_ref, rinv_ref, h_ref, out_ref):
    at = at_ref[0]
    members = h_ref.shape[0] * h_ref.shape[2]
    slots = cell_ref.shape[1]
    cell = cell_ref[pl.ds(at, 1), :]
    value = value_ref[pl.ds(at, 1), :]
    rinv = rinv_ref[pl.ds(at, 1), :]
    hx = jnp.zeros((members, slots), f32)
    for half in range(2):
        _, deviation = centred(h_ref[:, half])
        place = lax.broadcasted_iota(jnp.int32, (LANES, slots), 0) + half * LANES
        pick = jnp.where(place == cell, 1.0, 0.0).astype(bf16)
        hx = hx + jnp.dot(deviation, pick, preferred_element_type=f32)
    centre = jnp.sum(hx, axis=0, keepdims=True) * (1.0 / members)
    slot = lax.broadcasted_iota(jnp.int32, (1, slots), 1)
    weight = jnp.where(slot < count_ref[0, at], jnp.sqrt(rinv), 0.0)
    scaled = (weight * (hx - centre) * (1.0 / math.sqrt(members - 1))).astype(bf16)
    misfit = weight * (value - centre)
    summary = lax.dot_general(
        split3(misfit), scaled, (((1,), (1,)), ((), ())), preferred_element_type=f32
    )
    summary = jnp.sum(summary, axis=0, keepdims=True)
    out_ref[:members] = scaled
    pieces = [summary[:, i * LANES : (i + 1) * LANES] for i in range(members // LANES)]
    pieces.append(jnp.zeros((8 - len(pieces), LANES), f32))
    out_ref[members:] = jnp.concatenate(pieces, axis=0).astype(bf16)


def make_block(at, count, cell, value, rinv, h):
    members = h.shape[0] * h.shape[2]
    return pl.pallas_call(
        block_kernel,
        out_shape=jax.ShapeDtypeStruct((members + 8, cell.shape[1]), bf16),
        in_specs=[smem_spec(), smem_spec()] + [vmem_spec()] * 4,
        out_specs=vmem_spec(),
        name="block",
        compiler_params=pltpu.CompilerParams(vmem_limit_bytes=16 << 20),
    )(at, count, cell, value, rinv, h)


def transform_kernel(own_ref, west_ref, east_ref, north_ref, south_ref, out_ref):
    n = out_ref.shape[0]

    def gram_of(refs):
        y = jnp.concatenate([r[:n] for r in refs], axis=1)
        return lax.dot_general(y, y, (((1,), (1,)), ((), ())), preferred_element_type=f32)

    def drive_of(refs):
        total = refs[0][n:].astype(f32)
        for r in refs[1:]:
            total = total + r[n:].astype(f32)
        return total

    centre = [own_ref]
    edges = [west_ref, east_ref, north_ref.at[1], south_ref.at[1]]
    corners = [north_ref.at[0], north_ref.at[2], south_ref.at[0], south_ref.at[2]]
    drive = drive_of(centre) + EDGE_WEIGHT * drive_of(edges) + CORNER_WEIGHT * drive_of(corners)
    drive = jnp.concatenate([drive[i : i + 1] for i in range(n // LANES)], axis=1)
    gram = gram_of(centre) + EDGE_WEIGHT * gram_of(edges) + CORNER_WEIGHT * gram_of(corners)
    diagonal = lax.broadcasted_iota(jnp.int32, (n, n), 0) == lax.broadcasted_iota(jnp.int32, (n, n), 1)
    half_scale = 1.0 / NEWTON_SCALE
    root = (gram * half_scale + jnp.where(diagonal, half_scale, 0.0)).astype(bf16)
    shifted = jnp.where(diagonal, 1.5, 0.0)
    product = root.astype(f32)
    inverse = None
    for sweep in range(NS_ITERS):
        if sweep > 0:
            product = jnp.dot(root, inverse, preferred_element_type=f32)
        correction = (shifted - 0.5 * product).astype(bf16)
        if sweep + 1 < NS_ITERS:
            root = jnp.dot(correction, root, preferred_element_type=f32).astype(bf16)
        if sweep == 0:
            inverse = correction
        else:
            inverse = jnp.dot(inverse, correction, preferred_element_type=f32).astype(bf16)

    def apply(row):
        return jnp.sum(jnp.dot(split3(row), inverse, preferred_element_type=f32), axis=0, keepdims=True)

    weights = apply(apply(drive)) * (1.0 / NEWTON_SCALE / math.sqrt(n - 1))
    out_ref[...] = (weights + inverse.astype(f32) * (1.0 / math.sqrt(NEWTON_SCALE))).astype(bf16)


def make_transform(own, west, east, north, south):
    n = own.shape[0] - 8
    return pl.pallas_call(
        transform_kernel,
        out_shape=jax.ShapeDtypeStruct((n, n), bf16),
        in_specs=[vmem_spec()] * 5,
        out_specs=vmem_spec(),
        name="transform",
        compiler_params=pltpu.CompilerParams(vmem_limit_bytes=24 << 20),
    )(own, west, east, north, south)


def analysis_kernel(transform_ref, h_ref, uv_ref, out_ref):
    for f in range(3):
        src = h_ref if f == 0 else uv_ref
        for half in range(2):
            mean, deviation = centred(src[:, half + 2 * max(f - 1, 0)])
            out_ref[f, :, half * LANES : (half + 1) * LANES] = mean + jnp.dot(
                transform_ref[...], deviation, preferred_element_type=f32
            )


def analyse(transform, h, uv):
    n = transform.shape[0]
    return pl.pallas_call(
        analysis_kernel,
        out_shape=jax.ShapeDtypeStruct((3, n, EDGE * EDGE), f32),
        in_specs=[vmem_spec()] * 3,
        out_specs=vmem_spec(),
        name="analysis",
        compiler_params=pltpu.CompilerParams(vmem_limit_bytes=16 << 20),
    )(transform, h, uv)


def both_ways(before_part, after_part, axis):
    size = lax.axis_size(axis)
    up = [(i, i + 1) for i in range(size - 1)]
    down = [(j, i) for i, j in up]
    return lax.ppermute(after_part, axis, up), lax.ppermute(before_part, axis, down)


def per_device(ensemble_height_winds, obs_count, obs_cell, obs_value, obs_rinv):
    x = ensemble_height_winds
    at = lax.axis_index("mem").astype(jnp.int32).reshape(1)
    row = jnp.stack([lax.axis_index("lat"), lax.axis_size("lat")]).astype(jnp.int32)

    first, last = edge_rows(x)
    top, bottom = both_ways(first, last, "lat")
    s3, s1e, s2e = inner_forecast(x)
    h, uv = outer_forecast(row, top, first, last, bottom, s1e, s2e, s3)

    def exchange(part):
        return lax.all_to_all(part, "mem", split_axis=0, concat_axis=0, tiled=True)

    h = exchange(h)
    own = make_block(at, obs_count, obs_cell[0], obs_value[0], obs_rinv[0], h)
    uv, own = lax.optimization_barrier((uv, own))
    uv = exchange(uv)
    west, east = both_ways(own, own, "mem")
    line = jnp.stack([west, own, east])
    north, south = both_ways(line, line, "lat")
    transform = make_transform(own, west, east, north, south)
    analysed = analyse(transform, h, uv)
    return analysed.transpose(1, 0, 2)[None, None]


def solution(mesh):
    in_specs = (
        P("mem", None, "lat", None),
        P("lat", None),
        P("lat", None, None),
        P("lat", None, None),
        P("lat", None, None),
    )
    out_specs = P("lat", "mem", None, None, None)
    return jax.shard_map(
        per_device, mesh=mesh, in_specs=in_specs, out_specs=out_specs, check_vma=False
    )
```

time: 196 us -> 111 us (0.57)
  the two profiles are of different devices: /device:TPU:1 before, /device:TPU:34 now
where the time goes in v1:
time: 111 us; the launch traced here: 110 us
  waiting for transfers between devices  49.1 us (44%)
  starting transfers between devices  40.4 us (36%)
  Pallas kernels  19.1 us (17%)
  local copies, waits for them, and re-layouts  1.43 us (1%)
    all_to_all x2, starting transfers between devices, exchange(): return lax.all_to_all(part, 'mem', split_axis=0, concat_axis=0, tiled=True)  24 us
    all_to_all x2, waiting for transfers between devices, exchange(): return lax.all_to_all(part, 'mem', split_axis=0, concat_axis=0, tiled=True)  22.4 us
    ppermute x3, waiting for transfers between devices, both_ways(): lax.ppermute(before_part, axis, down)  20.4 us
    ppermute x3, starting transfers between devices, both_ways(): lax.ppermute(before_part, axis, down)  10.1 us
    ppermute x3, waiting for transfers between devices, both_ways(): lax.ppermute(after_part, axis, up)  6.38 us
    ppermute x3, starting transfers between devices, both_ways(): lax.ppermute(after_part, axis, up)  6.25 us
    pallas_call x1, Pallas kernels, inner_forecast(): pl.pallas_call(inner_kernel, out_shape=(part(rows - 2 * HALO), part(4), p...  5.43 us
    pallas_call x1, Pallas kernels, make_transform(): pl.pallas_call(transform_kernel, out_shape=jax.ShapeDtypeStruct((n, n), b...  5.01 us
  transfers between devices with their start and end apart: 8, of which 5 were waited for; matrix products, arithmetic and copies ran while one was open for 0% of the time, Pallas kernels for 9%

profile of v1, /device:TPU:34, one launch (start us, length us, event | category | flops | bytes accessed | tf_op | source)
XLA Modules:
  0.0 110.4 jit_solution(17713356734872344708)
XLA Ops:
  0.0 1.4 %copy-done = f32[8,3,16,1024]{3,2,1,0:T(8,128)S(1)} copy-done((f32[8,3,16,1024]{3,2,1,0:T(8,128)S(1)}, f32[8,3,16,1024]{3,2,1,0:T(8,128)}, u32[]{:S(2)}) %copy-start) | copy-done | bytes 1572888
  1.4 0.6 edges.1
  2.0 1.9 %collective-permute-start = (f32[3,3,8,1024]{3,2,1,0:T(8,128)S(1)}, f32[3,3,8,1024]{3,2,1,0:T(8,128)S(1)}, u32[]{:S(2)}, u32[]{:S(2)}) collective-permute-start(f32[3,3,8,1024]{3,2,1,0:T(8,128)S(1)} %get-tuple-element.14.last_ref), channel_id=1, source_target_pairs={{0,1},{1,2},{2,3},{3,4},{4,5},{5,6},{6,7},{8,9},{9,10},{10,11},{11... | collective-permute-start | bytes 884744 | tf_op jit(solution)/shard_map/ppermute | solution.py:385
  4.0 3.6 %collective-permute-start.1 = (f32[3,3,8,1024]{3,2,1,0:T(8,128)S(1)}, f32[3,3,8,1024]{3,2,1,0:T(8,128)S(1)}, u32[]{:S(2)}, u32[]{:S(2)}) collective-permute-start(f32[3,3,8,1024]{3,2,1,0:T(8,128)S(1)} %get-tuple-element.15.first_ref), channel_id=1, source_target_pairs={{1,0},{2,1},{3,2},{4,3},{5,4},{6,5},{7,6},{9,8},{10,9},{11,10},{12... | collective-permute-start | bytes 884744 | tf_op jit(solution)/shard_map/ppermute | solution.py:385
  7.6 5.4 %inner.1 = (f32[3,10,8,1024]{3,2,1,0:T(8,128)S(1)}, f32[3,4,8,1024]{3,2,1,0:T(8,128)S(1)}, f32[3,4,8,1024]{3,2,1,0:T(8,128)S(1)}) custom-call(f32[8,3,16,1024]{3,2,1,0:T(8,128)S(1)} %copy-done.1), custom_call_target="tpu_custom_call" | custom-call | flops 400000000 | bytes 4000000 | tf_op jit(solution)/shard_map/inner/pallas_call | solution.py:146
  13.1 0.1 pad_add_fusion.row_ref
  13.2 0.0 copy-start.3
  13.2 0.0 copy-start.4
  13.2 0.0 copy-start.5
  13.2 4.8 %outer.1 = (bf16[64,2,8,128]{3,2,1,0:T(8,128)(2,1)}, bf16[64,4,8,128]{3,2,1,0:T(8,128)(2,1)}) custom-call(s32[2]{0:T(128)S(1)} %pad_add_fusion.row_ref, f32[3,3,8,1024]{3,2,1,0:T(8,128)S(1)} %collective-permute-done.top_ref, f32[3,3,8,1024]{3,2,1,0:T(8,128)S(1)} %get-tuple-element.15.first_ref, f32[3,3,8,1024]{3,2,1,0:T(8,128)S(1)} %get-tuple-element.14.last_ref, ...), custom_call_target="tpu_custom_call" | custom-call | flops 200000000 | bytes 4000000 | tf_op jit(solution)/shard_map/outer/pallas_call | solution.py:234
  18.0 18.4 %all-to-all-start = ((bf16[64,2,8,128]{3,2,1,0:T(8,128)(2,1)}), bf16[64,2,8,128]{3,2,1,0:T(8,128)(2,1)S(1)}, u32[]{:S(2)}, u32[]{:S(2)}) async-start(bf16[64,2,8,128]{3,2,1,0:T(8,128)(2,1)} %get-tuple-element.20), calls=%async_computation | async-start | bytes 524288 | tf_op jit(solution)/shard_map/all_to_all | solution.py:399
  36.4 22.4 %all-to-all-done.h_ref = bf16[64,2,8,128]{3,2,1,0:T(8,128)(2,1)S(1)} async-done(((bf16[64,2,8,128]{3,2,1,0:T(8,128)(2,1)}), bf16[64,2,8,128]{3,2,1,0:T(8,128)(2,1)S(1)}, u32[]{:S(2)}, u32[]{:S(2)}) %all-to-all-start) | async-done | bytes 262176 | tf_op jit(solution)/shard_map/all_to_all | solution.py:399
  58.8 1.1 block.1.own_ref
  59.8 5.6 %all-to-all-start.1 = ((bf16[64,4,8,128]{3,2,1,0:T(8,128)(2,1)}), bf16[64,4,8,128]{3,2,1,0:T(8,128)(2,1)S(1)}, u32[]{:S(2)}, u32[]{:S(2)}) async-start(bf16[64,4,8,128]{3,2,1,0:T(8,128)(2,1)} %get-tuple-element.22), calls=%async_computation.1 | async-start | bytes 1048576 | tf_op jit(solution)/shard_map/all_to_all | solution.py:399
  65.5 4.6 %collective-permute-start.3 = (bf16[520,128]{1,0:T(8,128)(2,1)S(1)}, bf16[520,128]{1,0:T(8,128)(2,1)S(1)}, u32[]{:S(2)}, u32[]{:S(2)}) collective-permute-start(bf16[520,128]{1,0:T(8,128)(2,1)S(1)} %block.1.own_ref), channel_id=1, source_target_pairs={{8,0},{16,8},{24,16},{32,24},{40,32},{48,40},{56,48},{64,56},{72,6... | collective-permute-start | bytes 399368 | tf_op jit(solution)/shard_map/ppermute | solution.py:385
  70.1 1.9 %collective-permute-start.2 = (bf16[520,128]{1,0:T(8,128)(2,1)S(1)}, bf16[520,128]{1,0:T(8,128)(2,1)S(1)}, u32[]{:S(2)}, u32[]{:S(2)}) collective-permute-start(bf16[520,128]{1,0:T(8,128)(2,1)S(1)} %block.1.own_ref), channel_id=1, source_target_pairs={{0,8},{8,16},{16,24},{24,32},{32,40},{40,48},{48,56},{56,64},{64,7... | collective-permute-start | bytes 399368 | tf_op jit(solution)/shard_map/ppermute | solution.py:385
  72.0 17.5 %collective-permute-done.3.east_ref = bf16[520,128]{1,0:T(8,128)(2,1)S(1)} collective-permute-done((bf16[520,128]{1,0:T(8,128)(2,1)S(1)}, bf16[520,128]{1,0:T(8,128)(2,1)S(1)}, u32[]{:S(2)}, u32[]{:S(2)}) %collective-permute-start.3) | collective-permute-done | bytes 133152 | tf_op jit(solution)/shard_map/ppermute | solution.py:385
  89.5 2.6 %collective-permute-done.2.west_ref = bf16[520,128]{1,0:T(8,128)(2,1)S(1)} collective-permute-done((bf16[520,128]{1,0:T(8,128)(2,1)S(1)}, bf16[520,128]{1,0:T(8,128)(2,1)S(1)}, u32[]{:S(2)}, u32[]{:S(2)}) %collective-permute-start.2) | collective-permute-done | bytes 133152 | tf_op jit(solution)/shard_map/ppermute | solution.py:385
  92.0 1.9 %collective-permute-start.5 = (bf16[3,520,128]{2,1,0:T(8,128)(2,1)S(1)}, bf16[3,520,128]{2,1,0:T(8,128)(2,1)S(1)}, u32[]{:S(2)}, u32[]{:S(2)}) collective-permute-start(bf16[3,520,128]{2,1,0:T(8,128)(2,1)S(1)} %pad_maximum_fusion), channel_id=1, source_target_pairs={{1,0},{2,1},{3,2},{4,3},{5,4},{6,5},{7,6},{9,8},{10,9},{11,10},{12... | collective-permute-start | bytes 1198088 | tf_op jit(solution)/shard_map/ppermute | solution.py:385
  94.0 2.4 %collective-permute-start.4 = (bf16[3,520,128]{2,1,0:T(8,128)(2,1)S(1)}, bf16[3,520,128]{2,1,0:T(8,128)(2,1)S(1)}, u32[]{:S(2)}, u32[]{:S(2)}) collective-permute-start(bf16[3,520,128]{2,1,0:T(8,128)(2,1)S(1)} %pad_maximum_fusion), channel_id=1, source_target_pairs={{0,1},{1,2},{2,3},{3,4},{4,5},{5,6},{6,7},{8,9},{9,10},{10,11},{11... | collective-permute-start | bytes 1198088 | tf_op jit(solution)/shard_map/ppermute | solution.py:385
  96.4 2.9 %collective-permute-done.5.south_ref = bf16[3,520,128]{2,1,0:T(8,128)(2,1)S(1)} collective-permute-done((bf16[3,520,128]{2,1,0:T(8,128)(2,1)S(1)}, bf16[3,520,128]{2,1,0:T(8,128)(2,1)S(1)}, u32[]{:S(2)}, u32[]{:S(2)}) %collective-permute-start.5) | collective-permute-done | bytes 399392 | tf_op jit(solution)/shard_map/ppermute | solution.py:385
  99.3 3.8 %collective-permute-done.4.north_ref = bf16[3,520,128]{2,1,0:T(8,128)(2,1)S(1)} collective-permute-done((bf16[3,520,128]{2,1,0:T(8,128)(2,1)S(1)}, bf16[3,520,128]{2,1,0:T(8,128)(2,1)S(1)}, u32[]{:S(2)}, u32[]{:S(2)}) %collective-permute-start.4) | collective-permute-done | bytes 399392 | tf_op jit(solution)/shard_map/ppermute | solution.py:385
  103.1 5.0 %transform.1.transform_ref = bf16[512,512]{1,0:T(8,128)(2,1)S(1)} custom-call(bf16[520,128]{1,0:T(8,128)(2,1)S(1)} %block.1.own_ref, bf16[520,128]{1,0:T(8,128)(2,1)S(1)} %collective-permute-done.2.west_ref, bf16[520,128]{1,0:T(8,128)(2,1)S(1)} %collective-permute-done.3.east_ref, bf16[3,520,128]{2,1,0:T(8,128)(2,1)S(1)} %collective-permute-done.4.north_ref, ...), custom_call_target="tpu_custom_call" | custom-call | tf_op jit(solution)/shard_map/transform/pallas_call | solution.py:349
  108.2 2.2 %analysis.1 = f32[3,512,256]{2,1,0:T(8,128)} custom-call(bf16[512,512]{1,0:T(8,128)(2,1)S(1)} %transform.1.transform_ref, bf16[64,2,8,128]{3,2,1,0:T(8,128)(2,1)S(1)} %all-to-all-done.h_ref, bf16[64,4,8,128]{3,2,1,0:T(8,128)(2,1)S(1)} %all-to-all-done.1.uv_ref), custom_call_target="tpu_custom_call" | custom-call | tf_op jit(solution)/shard_map/analysis/pallas_call | solution.py:371
  (12 shorter events, 0.1 us)
Async XLA Ops:
  0.0 1.4 %copy-start = (f32[8,3,16,1024]{3,2,1,0:T(8,128)S(1)}, f32[8,3,16,1024]{3,2,1,0:T(8,128)}, u32[]{:S(2)}) copy-start(f32[8,3,16,1024]{3,2,1,0:T(8,128)} %x_ref.3) | copy-start | bytes 4718596
  1.4 6.2 %copy-start.1 = (f32[8,3,16,1024]{3,2,1,0:T(8,128)S(1)}, f32[8,3,16,1024]{3,2,1,0:T(8,128)}, u32[]{:S(2)}) copy-start(f32[8,3,16,1024]{3,2,1,0:T(8,128)} %x_ref.3) | copy-start | bytes 4718596
  2.0 11.1 %collective-permute-start = (f32[3,3,8,1024]{3,2,1,0:T(8,128)S(1)}, f32[3,3,8,1024]{3,2,1,0:T(8,128)S(1)}, u32[]{:S(2)}, u32[]{:S(2)}) collective-permute-start(f32[3,3,8,1024]{3,2,1,0:T(8,128)S(1)} %get-tuple-element.14.last_ref), channel_id=1, source_target_pairs={{0,1},{1,2},{2,3},{3,4},{4,5},{5,6},{6,7},{8,9},{9,10},{10,11},{11... | collective-permute-start | bytes 884744 | tf_op jit(solution)/shard_map/ppermute | solution.py:385
  4.0 9.2 %collective-permute-start.1 = (f32[3,3,8,1024]{3,2,1,0:T(8,128)S(1)}, f32[3,3,8,1024]{3,2,1,0:T(8,128)S(1)}, u32[]{:S(2)}, u32[]{:S(2)}) collective-permute-start(f32[3,3,8,1024]{3,2,1,0:T(8,128)S(1)} %get-tuple-element.15.first_ref), channel_id=1, source_target_pairs={{1,0},{2,1},{3,2},{4,3},{5,4},{6,5},{7,6},{9,8},{10,9},{11,10},{12... | collective-permute-start | bytes 884744 | tf_op jit(solution)/shard_map/ppermute | solution.py:385
  13.1 45.6 %copy-start.2 = (s32[1,64,128]{2,1,0:T(8,128)S(1)}, s32[1,64,128]{2,1,0:T(8,128)}, u32[]{:S(2)}) copy-start(s32[1,64,128]{2,1,0:T(8,128)} %param.7) | copy-start | bytes 98308
  13.2 45.6 %copy-start.3 = (f32[1,64,128]{2,1,0:T(8,128)S(1)}, f32[1,64,128]{2,1,0:T(8,128)}, u32[]{:S(2)}) copy-start(f32[1,64,128]{2,1,0:T(8,128)} %param.8) | copy-start | bytes 98308
  13.2 45.6 %copy-start.4 = (f32[1,64,128]{2,1,0:T(8,128)S(1)}, f32[1,64,128]{2,1,0:T(8,128)}, u32[]{:S(2)}) copy-start(f32[1,64,128]{2,1,0:T(8,128)} %param.9) | copy-start | bytes 98308
  13.2 45.6 %copy-start.5 = (s32[1,64]{1,0:T(1,128)S(1)}, s32[1,64]{1,0:T(1,128)}, u32[]{:S(2)}) copy-start(s32[1,64]{1,0:T(1,128)} %count_ref.1) | copy-start | bytes 772
  18.0 40.8 %all-to-all-start = ((bf16[64,2,8,128]{3,2,1,0:T(8,128)(2,1)}), bf16[64,2,8,128]{3,2,1,0:T(8,128)(2,1)S(1)}, u32[]{:S(2)}, u32[]{:S(2)}) async-start(bf16[64,2,8,128]{3,2,1,0:T(8,128)(2,1)} %get-tuple-element.20), calls=%async_computation | async-start | bytes 524288 | tf_op jit(solution)/shard_map/all_to_all | solution.py:399
  59.8 48.3 %all-to-all-start.1 = ((bf16[64,4,8,128]{3,2,1,0:T(8,128)(2,1)}), bf16[64,4,8,128]{3,2,1,0:T(8,128)(2,1)S(1)}, u32[]{:S(2)}, u32[]{:S(2)}) async-start(bf16[64,4,8,128]{3,2,1,0:T(8,128)(2,1)} %get-tuple-element.22), calls=%async_computation.1 | async-start | bytes 1048576 | tf_op jit(solution)/shard_map/all_to_all | solution.py:399
  65.5 24.0 %collective-permute-start.3 = (bf16[520,128]{1,0:T(8,128)(2,1)S(1)}, bf16[520,128]{1,0:T(8,128)(2,1)S(1)}, u32[]{:S(2)}, u32[]{:S(2)}) collective-permute-start(bf16[520,128]{1,0:T(8,128)(2,1)S(1)} %block.1.own_ref), channel_id=1, source_target_pairs={{8,0},{16,8},{24,16},{32,24},{40,32},{48,40},{56,48},{64,56},{72,6... | collective-permute-start | bytes 399368 | tf_op jit(solution)/shard_map/ppermute | solution.py:385
  70.1 21.9 %collective-permute-start.2 = (bf16[520,128]{1,0:T(8,128)(2,1)S(1)}, bf16[520,128]{1,0:T(8,128)(2,1)S(1)}, u32[]{:S(2)}, u32[]{:S(2)}) collective-permute-start(bf16[520,128]{1,0:T(8,128)(2,1)S(1)} %block.1.own_ref), channel_id=1, source_target_pairs={{0,8},{8,16},{16,24},{24,32},{32,40},{40,48},{48,56},{56,64},{64,7... | collective-permute-start | bytes 399368 | tf_op jit(solution)/shard_map/ppermute | solution.py:385
  92.0 7.3 %collective-permute-start.5 = (bf16[3,520,128]{2,1,0:T(8,128)(2,1)S(1)}, bf16[3,520,128]{2,1,0:T(8,128)(2,1)S(1)}, u32[]{:S(2)}, u32[]{:S(2)}) collective-permute-start(bf16[3,520,128]{2,1,0:T(8,128)(2,1)S(1)} %pad_maximum_fusion), channel_id=1, source_target_pairs={{1,0},{2,1},{3,2},{4,3},{5,4},{6,5},{7,6},{9,8},{10,9},{11,10},{12... | collective-permute-start | bytes 1198088 | tf_op jit(solution)/shard_map/ppermute | solution.py:385
  94.0 9.2 %collective-permute-start.4 = (bf16[3,520,128]{2,1,0:T(8,128)(2,1)S(1)}, bf16[3,520,128]{2,1,0:T(8,128)(2,1)S(1)}, u32[]{:S(2)}, u32[]{:S(2)}) collective-permute-start(bf16[3,520,128]{2,1,0:T(8,128)(2,1)S(1)} %pad_maximum_fusion), channel_id=1, source_target_pairs={{0,1},{1,2},{2,3},{3,4},{4,5},{5,6},{6,7},{8,9},{9,10},{10,11},{11... | collective-permute-start | bytes 1198088 | tf_op jit(solution)/shard_map/ppermute | solution.py:385

commit v2 on v1

v2 whole, which is shorter than its diff:
```python
import functools
import math


import jax
import jax.numpy as jnp
from jax import lax
from jax.experimental import pallas as pl
from jax.experimental.pallas import tpu as pltpu
from jax.sharding import PartitionSpec as P

EDGE = 16
NS_ITERS = 5
EDGE_WEIGHT = 0.6
CORNER_WEIGHT = 0.35
NEWTON_SCALE = 16.0
HALO = 3
RING = 4
LANES = 128

bf16 = jnp.bfloat16
f32 = jnp.float32


def vmem_spec():
    return pl.BlockSpec(memory_space=pltpu.VMEM)


def smem_spec():
    return pl.BlockSpec(memory_space=pltpu.SMEM)


def tile_shifts(load, n, lane):
    tiles, ahead, behind = {}, {}, {}

    def get(t):
        if t not in tiles:
            tiles[t] = load(t)
            ahead[t] = pltpu.roll(tiles[t], LANES - 1, 1)
            behind[t] = pltpu.roll(tiles[t], 1, 1)

    def at(t):
        get(t)
        if t + 1 < n:
            get(t + 1)
        edge = ahead[t + 1] if t + 1 < n else jnp.zeros_like(tiles[t])
        plus = jnp.where(lane == LANES - 1, edge, ahead[t])
        edge = behind[t - 1] if t > 0 else jnp.zeros_like(tiles[t])
        minus = jnp.where(lane == 0, edge, behind[t])
        return tiles[t], plus - minus

    return at


def advance(src, i, lane, n_tiles, fields=(0, 1, 2)):
    def load(f, k):
        return lambda t: src[f, k, :, t * LANES : (t + 1) * LANES]

    h_at = tile_shifts(load(0, i), n_tiles, lane)
    u_at = tile_shifts(load(1, i), n_tiles, lane)
    v_at = tile_shifts(load(2, i), n_tiles, lane)
    flux_at = tile_shifts(
        lambda t: (1.0 + load(0, i)(t)) * load(1, i)(t), n_tiles, lane
    )
    for t in range(n_tiles):
        hu, hd = load(0, i + 1)(t), load(0, i - 1)(t)
        vu, vd = load(2, i + 1)(t), load(2, i - 1)(t)
        new = []
        if 0 in fields:
            _, df = flux_at(t)
            dyf = (1.0 + hu) * vu - (1.0 + hd) * vd
            new.append(load(0, i)(t) - 0.25 * (df + dyf))
        if 1 in fields:
            _, dh = h_at(t)
            u, du = u_at(t)
            v, dv = v_at(t)
            dyu = load(1, i + 1)(t) - load(1, i - 1)(t)
            qu, qv = 0.25 * u, 0.25 * v
            new.append(u - (qu * du + qv * (dyu - 0.5) + 0.25 * dh))
            new.append(v - (qu * (dv + 0.5) + qv * (vu - vd) + 0.25 * (hu - hd)))
        yield t, new


def edge_kernel(row_ref, q_ref, near_ref, far_ref):
    rows = q_ref.shape[1]

    def place(first_ref, last_ref):
        first_ref[...] = q_ref[:, :HALO]
        last_ref[...] = q_ref[:, rows - HALO :]

    @pl.when(row_ref[0] % 2 == 0)
    def _():
        place(far_ref, near_ref)

    @pl.when(row_ref[0] % 2 == 1)
    def _():
        place(near_ref, far_ref)


def edge_rows(row, q):
    fields, _, members, columns = q.shape
    part = jax.ShapeDtypeStruct((fields, HALO, members, columns), f32)
    return pl.pallas_call(
        edge_kernel,
        out_shape=(part, part),
        in_specs=[smem_spec(), vmem_spec()],
        out_specs=(vmem_spec(), vmem_spec()),
        compiler_params=pltpu.CompilerParams(vmem_limit_bytes=4 << 20),
        name="edges",
    )(row, q)


def inner_kernel(q, s3_ref, s1e_ref, s2e_ref, a, b):
    rows = q.shape[1]
    n_tiles = q.shape[3] // LANES
    lane = lax.broadcasted_iota(jnp.int32, (8, LANES), 1)

    def section(src, dst, lo, hi, off, combine):
        @pl.loop(lo, hi, unroll=2)
        def _(i):
            for t, new in advance(src, i, lane, n_tiles):
                sl = slice(t * LANES, (t + 1) * LANES)
                for f in range(3):
                    dst[f, i - off, :, sl] = combine(new[f], lambda: q[f, i, :, sl])

    section(q, a, 1, rows - 1, 0, lambda s, q0: s)
    section(a, b, 2, rows - 2, 0, lambda s, q0: 0.75 * q0() + 0.25 * s)
    section(b, s3_ref, 3, rows - 3, 3, lambda s, q0: q0() * (1.0 / 3.0) + (2.0 / 3.0) * s)
    s1e_ref[:, :2] = a[:, 1:3]
    s1e_ref[:, 2:] = a[:, rows - 3 : rows - 1]
    s2e_ref[:, :2] = b[:, 2:4]
    s2e_ref[:, 2:] = b[:, rows - 4 : rows - 2]


def inner_forecast(q):
    fields, rows, members, columns = q.shape

    def part(n):
        return jax.ShapeDtypeStruct((fields, n, members, columns), f32)

    return pl.pallas_call(
        inner_kernel,
        out_shape=(part(rows - 2 * HALO), part(4), part(4)),
        in_specs=[vmem_spec()],
        out_specs=(vmem_spec(),) * 3,
        scratch_shapes=[pltpu.VMEM((fields, rows, members, columns), f32)] * 2,
        compiler_params=pltpu.CompilerParams(vmem_limit_bytes=12 << 20),
        cost_estimate=pl.CostEstimate(flops=4 * 10**8, bytes_accessed=4 * 10**6, transcendentals=0),
        name="inner",
    )(q)


def edge_section(src, dst, lane, n_tiles, fields, places, combine):
    @pl.loop(0, 2 * HALO, unroll=2 * HALO)
    def _(i):
        at, to, q_row = places(i, (i >= HALO).astype(jnp.int32))
        for t, new in advance(src, at, lane, n_tiles, fields):
            sl = slice(t * LANES, (t + 1) * LANES)
            for k, f in enumerate(fields):
                dst[f - fields[0], to, :, sl] = combine(new[k], lambda: q_row(f, sl))


def final_section(lane, n_tiles, fields, q_row, b, c):
    for i in range(2 * HALO):
        at = i + 1 if i < HALO else i + 3
        for t, new in advance(b, at, lane, n_tiles, fields):
            sl = slice(t * LANES, (t + 1) * LANES)
            for k, f in enumerate(fields):
                c[f - fields[0], i, :, sl] = q_row(f, i, sl) * (1.0 / 3.0) + (2.0 / 3.0) * new[k]


def regroup(lane, n_tiles, fields, s3_ref, c, store):
    rows = s3_ref.shape[1] + 2 * HALO
    block = lane // EDGE
    keep = {bit: (block & bit) == 0 for bit in (1, 2, 4)}

    def final_row(f, r, col):
        if r < HALO:
            return c[f - fields[0], r, :, col]
        if r >= rows - HALO:
            return c[f - fields[0], r - rows + 2 * HALO, :, col]
        return s3_ref[f, r - HALO, :, col]

    @pl.loop(0, n_tiles)
    def _(t):
        col = pl.ds(pl.multiple_of(t * LANES, LANES), LANES)
        for f in fields:
            for half in range(rows // 8):
                v = [final_row(f, half * 8 + r, col) for r in range(8)]
                for bit in (4, 2, 1):
                    for i in range(8):
                        if i & bit:
                            continue
                        lo, hi = v[i], v[i | bit]
                        v[i] = jnp.where(keep[bit], lo, pltpu.roll(hi, bit * EDGE, 1))
                        v[i | bit] = jnp.where(keep[bit], pltpu.roll(lo, LANES - bit * EDGE, 1), hi)
                for d in range(8):
                    store(t, d, (f - fields[0]) * 2 + half, v[d].astype(bf16))


def outer_height_kernel(
    n_rows,
    row_ref,
    near_ref,
    far_ref,
    from_near_ref,
    from_far_ref,
    s1e_ref,
    s2e_ref,
    s3_ref,
    h_ref,
    b,
    q,
    a,
    c,
):
    n_tiles = s3_ref.shape[3] // LANES
    lane = lax.broadcasted_iota(jnp.int32, (8, LANES), 1)

    def place(top_ref, first_ref, last_ref, bottom_ref):
        q[:, 0:3] = top_ref[...]
        q[:, 3:6] = first_ref[...]
        q[:, 6:9] = last_ref[...]
        q[:, 9:12] = bottom_ref[...]
        b[:, 10:13] = first_ref[...]
        b[:, 13:16] = last_ref[...]

    @pl.when(row_ref[0] % 2 == 0)
    def _():
        place(from_far_ref, far_ref, near_ref, from_near_ref)

    @pl.when(row_ref[0] % 2 == 1)
    def _():
        place(from_near_ref, near_ref, far_ref, from_far_ref)

    a[:, 3:7] = s1e_ref[...]
    b[:, 3:7] = s2e_ref[...]

    def q_row(k):
        return lambda f, sl: q[f, k, :, sl]

    def clear(ref, top_at, bottom_at):
        @pl.when(row_ref[0] == 0)
        def _():
            ref[:, top_at] = jnp.zeros_like(ref[:, top_at])

        @pl.when(row_ref[0] == n_rows - 1)
        def _():
            ref[:, bottom_at] = jnp.zeros_like(ref[:, bottom_at])

    every = (0, 1, 2)
    edge_section(
        q, a, lane, n_tiles, every, lambda i, low: (i + 1 + 4 * low, i + 4 * low, None), lambda s, q0: s
    )
    clear(a, 1, 8)
    edge_section(
        a,
        b,
        lane,
        n_tiles,
        every,
        lambda i, low: (i + 1 + 2 * low, i + 4 * low, q_row(i + 2 + 2 * low)),
        lambda s, q0: 0.75 * q0() + 0.25 * s,
    )
    clear(b, 0, 9)
    final_section(lane, n_tiles, (0,), lambda f, i, sl: b[f, 10 + i, :, sl], b, c)

    def store(t, d, k, cells):
        h_ref[t * 8 + d, k] = cells

    regroup(lane, n_tiles, (0,), s3_ref, c, store)


def outer_wind_kernel(at_ref, b_ref, s3_ref, uv_ref, c):
    n_tiles = s3_ref.shape[3] // LANES
    lane = lax.broadcasted_iota(jnp.int32, (8, LANES), 1)
    final_section(lane, n_tiles, (1, 2), lambda f, i, sl: b_ref[f, 10 + i, :, sl], b_ref, c)
    ring = at_ref[0] % RING

    def store(t, d, k, cells):
        uv_ref[(d % RING) ^ ring, t * (8 // RING) + d // RING, k] = cells

    regroup(lane, n_tiles, (1, 2), s3_ref, c, store)


def outer_heights(row, near, far, from_near, from_far, s1e, s2e, s3):
    fields, _, members, columns = s3.shape
    n_dest = columns // EDGE

    def scratch(f, n):
        return pltpu.VMEM((f, n, members, columns), f32)

    return pl.pallas_call(
        functools.partial(outer_height_kernel, lax.axis_size("lat")),
        out_shape=(
            jax.ShapeDtypeStruct((n_dest, 2, members, LANES), bf16),
            jax.ShapeDtypeStruct((fields, 16, members, columns), f32),
        ),
        in_specs=[smem_spec()] + [vmem_spec()] * 7,
        out_specs=(vmem_spec(), vmem_spec()),
        scratch_shapes=[
            scratch(fields, 12),
            scratch(fields, 10),
            scratch(1, 6),
        ],
        compiler_params=pltpu.CompilerParams(vmem_limit_bytes=16 << 20),
        cost_estimate=pl.CostEstimate(flops=2 * 10**8, bytes_accessed=4 * 10**6, transcendentals=0),
        name="outer_heights",
    )(row, near, far, from_near, from_far, s1e, s2e, s3)


def outer_winds(at, b, s3):
    _, _, members, columns = s3.shape
    return pl.pallas_call(
        outer_wind_kernel,
        out_shape=jax.ShapeDtypeStruct((RING, columns // EDGE // RING, 4, members, LANES), bf16),
        in_specs=[smem_spec()] + [vmem_spec()] * 2,
        out_specs=vmem_spec(),
        scratch_shapes=[pltpu.VMEM((2, 2 * HALO, members, columns), f32)],
        compiler_params=pltpu.CompilerParams(vmem_limit_bytes=12 << 20),
        cost_estimate=pl.CostEstimate(flops=10**8, bytes_accessed=4 * 10**6, transcendentals=0),
        name="outer_winds",
    )(at, b, s3)


def ring_kernel(at_ref, *refs):
    out_ref = refs[-1]
    ring = at_ref[0] % RING
    for s, ref in enumerate(refs[:-1]):
        out_ref[:, ring ^ s] = ref[...]


def ring_line(at, pieces):
    first, *rest = pieces[0].shape
    return pl.pallas_call(
        ring_kernel,
        out_shape=jax.ShapeDtypeStruct((first, RING, *rest), bf16),
        in_specs=[smem_spec()] + [vmem_spec()] * RING,
        out_specs=vmem_spec(),
        compiler_params=pltpu.CompilerParams(vmem_limit_bytes=4 << 20),
        name="ring",
    )(at, *pieces)


def split3(row):
    high = row.astype(bf16)
    rest = row - high.astype(f32)
    mid = rest.astype(bf16)
    low = (rest - mid.astype(f32)).astype(bf16)
    zero = jnp.zeros((5, row.shape[1]), f32)
    return jnp.concatenate([high.astype(f32), mid.astype(f32), low.astype(f32), zero], axis=0).astype(bf16)


def centred(slab):
    value = slab.astype(f32).reshape(-1, LANES)
    mean = jnp.sum(value, axis=0, keepdims=True) * (1.0 / value.shape[0])
    return mean, (value - mean).astype(bf16)


def prepare_kernel(at_ref, count_ref, cell_ref, value_ref, rinv_ref, pick_ref, weight_ref):
    at = at_ref[0]
    cells, slots = pick_ref.shape
    place = lax.broadcasted_iota(jnp.int32, (cells, slots), 0)
    pick_ref[...] = jnp.where(place == cell_ref[pl.ds(at, 1), :], 1.0, 0.0).astype(bf16)
    slot = lax.broadcasted_iota(jnp.int32, (1, slots), 1)
    weight = jnp.where(slot < count_ref[0, at], jnp.sqrt(rinv_ref[pl.ds(at, 1), :]), 0.0)
    weight_ref[0:1] = weight
    weight_ref[1:2] = value_ref[pl.ds(at, 1), :]


def prepare(at, count, cell, value, rinv):
    slots = cell.shape[1]
    return pl.pallas_call(
        prepare_kernel,
        out_shape=(
            jax.ShapeDtypeStruct((EDGE * EDGE, slots), bf16),
            jax.ShapeDtypeStruct((2, slots), f32),
        ),
        in_specs=[smem_spec(), smem_spec()] + [vmem_spec()] * 3,
        out_specs=(vmem_spec(), vmem_spec()),
        compiler_params=pltpu.CompilerParams(vmem_limit_bytes=4 << 20),
        name="prepare",
    )(at, count, cell, value, rinv)


def block_kernel(pick_ref, weight_ref, h_ref, out_ref):
    members = h_ref.shape[0] * h_ref.shape[2]
    slots = pick_ref.shape[1]
    weight = weight_ref[0:1]
    hx = jnp.zeros((members, slots), f32)
    for half in range(2):
        _, deviation = centred(h_ref[:, half])
        pick = pick_ref[half * LANES : (half + 1) * LANES]
        hx = hx + jnp.dot(deviation, pick, preferred_element_type=f32)
    centre = jnp.sum(hx, axis=0, keepdims=True) * (1.0 / members)
    scaled = (weight * (hx - centre) * (1.0 / math.sqrt(members - 1))).astype(bf16)
    misfit = weight * (weight_ref[1:2] - centre)
    summary = lax.dot_general(
        split3(misfit), scaled, (((1,), (1,)), ((), ())), preferred_element_type=f32
    )
    summary = jnp.sum(summary, axis=0, keepdims=True)
    out_ref[:members] = scaled
    pieces = [summary[:, i * LANES : (i + 1) * LANES] for i in range(members // LANES)]
    pieces.append(jnp.zeros((8 - len(pieces), LANES), f32))
    out_ref[members:] = jnp.concatenate(pieces, axis=0).astype(bf16)


def make_block(pick, weight, h):
    members = h.shape[0] * h.shape[2]
    return pl.pallas_call(
        block_kernel,
        out_shape=jax.ShapeDtypeStruct((members + 8, pick.shape[1]), bf16),
        in_specs=[vmem_spec()] * 3,
        out_specs=vmem_spec(),
        compiler_params=pltpu.CompilerParams(vmem_limit_bytes=16 << 20),
        name="block",
    )(pick, weight, h)


def stack_kernel(west_ref, own_ref, east_ref, out_ref):
    for k, ref in enumerate((west_ref, own_ref, east_ref)):
        out_ref[k] = ref[...]


def stack_line(west, own, east):
    return pl.pallas_call(
        stack_kernel,
        out_shape=jax.ShapeDtypeStruct((3,) + own.shape, own.dtype),
        in_specs=[vmem_spec()] * 3,
        out_specs=vmem_spec(),
        compiler_params=pltpu.CompilerParams(vmem_limit_bytes=4 << 20),
        name="line",
    )(west, own, east)


def transform_kernel(own_ref, west_ref, east_ref, north_ref, south_ref, out_ref):
    n = out_ref.shape[0]

    def gram_of(refs):
        y = jnp.concatenate([r[:n] for r in refs], axis=1)
        return lax.dot_general(y, y, (((1,), (1,)), ((), ())), preferred_element_type=f32)

    def drive_of(refs):
        total = refs[0][n:].astype(f32)
        for r in refs[1:]:
            total = total + r[n:].astype(f32)
        return total

    centre = [own_ref]
    edges = [west_ref, east_ref, north_ref.at[1], south_ref.at[1]]
    corners = [north_ref.at[0], north_ref.at[2], south_ref.at[0], south_ref.at[2]]
    drive = drive_of(centre) + EDGE_WEIGHT * drive_of(edges) + CORNER_WEIGHT * drive_of(corners)
    drive = jnp.concatenate([drive[i : i + 1] for i in range(n // LANES)], axis=1)
    gram = gram_of(centre) + EDGE_WEIGHT * gram_of(edges) + CORNER_WEIGHT * gram_of(corners)
    diagonal = lax.broadcasted_iota(jnp.int32, (n, n), 0) == lax.broadcasted_iota(jnp.int32, (n, n), 1)
    half_scale = 1.0 / NEWTON_SCALE
    root = (gram * half_scale + jnp.where(diagonal, half_scale, 0.0)).astype(bf16)
    shifted = jnp.where(diagonal, 1.5, 0.0)
    product = root.astype(f32)
    inverse = None
    for sweep in range(NS_ITERS):
        if sweep > 0:
            product = jnp.dot(root, inverse, preferred_element_type=f32)
        correction = (shifted - 0.5 * product).astype(bf16)
        if sweep + 1 < NS_ITERS:
            root = jnp.dot(correction, root, preferred_element_type=f32).astype(bf16)
        if sweep == 0:
            inverse = correction
        else:
            inverse = jnp.dot(inverse, correction, preferred_element_type=f32).astype(bf16)

    def apply(row):
        return jnp.sum(jnp.dot(split3(row), inverse, preferred_element_type=f32), axis=0, keepdims=True)

    weights = apply(apply(drive)) * (1.0 / NEWTON_SCALE / math.sqrt(n - 1))
    out_ref[...] = (weights + inverse.astype(f32) * (1.0 / math.sqrt(NEWTON_SCALE))).astype(bf16)


def make_transform(own, west, east, north, south):
    n = own.shape[0] - 8
    return pl.pallas_call(
        transform_kernel,
        out_shape=jax.ShapeDtypeStruct((n, n), bf16),
        in_specs=[vmem_spec()] * 5,
        out_specs=vmem_spec(),
        name="transform",
        compiler_params=pltpu.CompilerParams(vmem_limit_bytes=24 << 20),
    )(own, west, east, north, south)


def analysed_field(transform_ref, slab, f, out_ref, buffer, sems, at):
    for half in range(2):
        mean, deviation = centred(slab(half))
        buffer[f, :, half * LANES : (half + 1) * LANES] = mean + jnp.dot(
            transform_ref[...], deviation, preferred_element_type=f32
        )
    copy = pltpu.make_async_copy(buffer.at[f], out_ref.at[at], sems.at[f])
    copy.start()
    return copy


def height_kernel(transform_ref, h_ref, out_ref, buffer, sems):
    analysed_field(transform_ref, lambda half: h_ref[:, half], 0, out_ref, buffer, sems, 0).wait()


def wind_kernel(transform_ref, uv_ref, _, out_ref, buffer, sems):
    copies = [
        analysed_field(
            transform_ref, lambda half, f=f: uv_ref[:, 2 * f + half], f, out_ref, buffer, sems, f + 1
        )
        for f in range(2)
    ]
    for c in copies:
        c.wait()


def analyse(transform, h, uv_of):
    n = transform.shape[0]
    cells = EDGE * EDGE
    shape = jax.ShapeDtypeStruct((3, n, cells), f32)
    hbm = pl.BlockSpec(memory_space=pltpu.HBM)
    params = pltpu.CompilerParams(vmem_limit_bytes=8 << 20)
    part = pl.pallas_call(
        height_kernel,
        out_shape=shape,
        in_specs=[vmem_spec()] * 2,
        out_specs=hbm,
        scratch_shapes=[pltpu.VMEM((1, n, cells), f32), pltpu.SemaphoreType.DMA((1,))],
        compiler_params=params,
        cost_estimate=pl.CostEstimate(flops=2 * n * n * cells, bytes_accessed=10**6, transcendentals=0),
        name="heights",
    )(transform, h)
    return pl.pallas_call(
        wind_kernel,
        out_shape=shape,
        in_specs=[vmem_spec()] * 2 + [hbm],
        out_specs=hbm,
        scratch_shapes=[pltpu.VMEM((2, n, cells), f32), pltpu.SemaphoreType.DMA((2,))],
        input_output_aliases={2: 0},
        compiler_params=params,
        name="wind_analysis",
    )(transform, uv_of, part)


def swap(part, axis, start):
    size = lax.axis_size(axis)
    pairs = [(i, i + 1) for i in range(start, size - 1, 2)]
    return lax.ppermute(part, axis, pairs + [(j, i) for i, j in pairs])


def per_device(ensemble_height_winds, obs_count, obs_cell, obs_value, obs_rinv):
    at = lax.axis_index("mem").astype(jnp.int32).reshape(1)
    row = lax.axis_index("lat").astype(jnp.int32).reshape(1)

    q = ensemble_height_winds.transpose(1, 2, 0, 3)
    near, far = edge_rows(row, q)
    from_near = swap(near, "lat", 0)
    from_far = swap(far, "lat", 1)
    s3, s1e, s2e = inner_forecast(q)
    h, edge = outer_heights(row, near, far, from_near, from_far, s1e, s2e, s3)
    uv = outer_winds(at, edge, s3)

    size = lax.axis_size("mem")

    def around(part, shift):
        return lax.ppermute(
            part, "mem", [(i, i ^ shift) for i in range(size)]
        )

    def exchange(part):
        return lax.all_to_all(part, "mem", split_axis=0, concat_axis=0, tiled=True)

    h = exchange(h)
    pick, weight = prepare(at, obs_count, obs_cell[0], obs_value[0], obs_rinv[0])
    own = make_block(pick, weight, h)
    pieces = [uv[0]] + [around(uv[s], s) for s in range(1, RING)]
    uv = ring_line(at, pieces)
    uv = lax.all_to_all(
        uv,
        "mem",
        split_axis=0,
        concat_axis=0,
        axis_index_groups=[list(range(i, size, RING)) for i in range(RING)],
        tiled=True,
    ).reshape(h.shape[0], 4, *h.shape[2:])
    west = swap(own, "mem", 1)
    east = swap(own, "mem", 0)
    line = stack_line(west, own, east)
    north = swap(line, "lat", 1)
    south = swap(line, "lat", 0)
    transform = make_transform(own, west, east, north, south)
    analysed = analyse(transform, h, uv)
    return analysed.transpose(1, 0, 2)[None, None]


def solution(mesh):
    in_specs = (
        P("mem", None, "lat", None),
        P("lat", None),
        P("lat", None, None),
        P("lat", None, None),
        P("lat", None, None),
    )
    out_specs = P("lat", "mem", None, None, None)
    return jax.shard_map(
        per_device, mesh=mesh, in_specs=in_specs, out_specs=out_specs, check_vma=False
    )
```

time: 111 us -> 111 us (level)
  the two profiles are of different devices: /device:TPU:34 before, /device:TPU:67 now
where the time goes in v2:
time: 111 us
  starting transfers between devices  55.8 us (50%)
  waiting for transfers between devices  32.5 us (29%)
  Pallas kernels  19.7 us (18%)
  local copies, waits for them, and re-layouts  2.38 us (2%)
    ppermute x6, waiting for transfers between devices, swap(): return lax.ppermute(part, axis, pairs + [(j, i) for i, j in pairs])  27.7 us
    ppermute x6, starting transfers between devices, swap(): return lax.ppermute(part, axis, pairs + [(j, i) for i, j in pairs])  18.6 us
    all_to_all x1, starting transfers between devices, exchange(): return lax.all_to_all(part, 'mem', split_axis=0, concat_axis=0, tiled=True)  17.4 us
    all_to_all x1, starting transfers between devices, per_device(): lax.all_to_all(uv, 'mem', split_axis=0, concat_axis=0, axis_index_groups=...  10.9 us
    ppermute x3, starting transfers between devices, around(): return lax.ppermute(part, 'mem', [(i, i ^ shift) for i in range(size)])  8.98 us
    pallas_call x1, Pallas kernels, make_transform(): pl.pallas_call(transform_kernel, out_shape=jax.ShapeDtypeStruct((n, n), b...  5.01 us
    ppermute x3, waiting for transfers between devices, around(): return lax.ppermute(part, 'mem', [(i, i ^ shift) for i in range(size)])  4.69 us
    pallas_call x1, Pallas kernels, inner_forecast(): pl.pallas_call(inner_kernel, out_shape=(part(rows - 2 * HALO), part(4), p...  3.78 us
  transfers between devices with their start and end apart: 11, of which 6 were waited for; matrix products, arithmetic and copies ran while one was open for 0% of the time, Pallas kernels for 13%

profile of v2, /device:TPU:67, one launch (start us, length us, event | category | flops | bytes accessed | tf_op | source)
XLA Modules:
  0.0 110.6 jit_solution(8587730977322422946)
XLA Ops:
  0.0 2.3 %copy.9 = f32[8,3,16,1024]{3,0,2,1:T(8,128)S(1)} copy(f32[8,3,16,1024]{3,2,1,0:T(8,128)} %param.5) | data formatting | bytes 3145728 | tf_op args[0]
  2.4 2.6 %collective-permute-start = (f32[3,3,8,1024]{3,2,1,0:T(8,128)S(1)}, f32[3,3,8,1024]{3,2,1,0:T(8,128)S(1)}, u32[]{:S(2)}, u32[]{:S(2)}) collective-permute-start(f32[3,3,8,1024]{3,2,1,0:T(8,128)S(1)} %get-tuple-element.16.near_ref), channel_id=1, source_target_pairs={{0,1},{2,3},{4,5},{6,7},{1,0},{3,2},{5,4},{7,6},{8,9},{10,11},{12,... | collective-permute-start | bytes 884744 | tf_op jit(solution)/shard_map/ppermute | solution.py:548
  5.0 3.0 %collective-permute-start.1 = (f32[3,3,8,1024]{3,2,1,0:T(8,128)S(1)}, f32[3,3,8,1024]{3,2,1,0:T(8,128)S(1)}, u32[]{:S(2)}, u32[]{:S(2)}) collective-permute-start(f32[3,3,8,1024]{3,2,1,0:T(8,128)S(1)} %get-tuple-element.17.far_ref), channel_id=1, source_target_pairs={{1,2},{3,4},{5,6},{2,1},{4,3},{6,5},{9,10},{11,12},{13,14},{10,9},... | collective-permute-start | bytes 884744 | tf_op jit(solution)/shard_map/ppermute | solution.py:548
  8.0 3.8 %inner.1 = (f32[3,10,8,1024]{3,2,1,0:T(8,128)S(1)}, f32[3,4,8,1024]{3,2,1,0:T(8,128)S(1)}, f32[3,4,8,1024]{3,2,1,0:T(8,128)S(1)}) custom-call(f32[3,16,8,1024]{3,2,1,0:T(8,128)S(1)} %bitcast.21), custom_call_target="tpu_custom_call" | custom-call | flops 400000000 | bytes 4000000 | tf_op jit(solution)/shard_map/inner/pallas_call | solution.py:141
  11.8 1.2 %collective-permute-done.1.from_far_ref = f32[3,3,8,1024]{3,2,1,0:T(8,128)S(1)} collective-permute-done((f32[3,3,8,1024]{3,2,1,0:T(8,128)S(1)}, f32[3,3,8,1024]{3,2,1,0:T(8,128)S(1)}, u32[]{:S(2)}, u32[]{:S(2)}) %collective-permute-start.1) | collective-permute-done | bytes 294944 | tf_op jit(solution)/shard_map/ppermute | solution.py:548
  13.0 3.7 %outer_heights.1 = (bf16[64,2,8,128]{3,2,1,0:T(8,128)(2,1)}, f32[3,16,8,1024]{3,2,1,0:T(8,128)S(1)}) custom-call(s32[1]{0:T(128)} %bitcast.4.row_ref, f32[3,3,8,1024]{3,2,1,0:T(8,128)S(1)} %get-tuple-element.16.near_ref, f32[3,3,8,1024]{3,2,1,0:T(8,128)S(1)} %get-tuple-element.17.far_ref, f32[3,3,8,1024]{3,2,1,0:T(8,128)S(1)} %collective-permute-done.from_near_ref, ...), custom_call_target="tpu_custom_call" | custom-call | flops 200000000 | bytes 4000000 | tf_op jit(solution)/shard_map/outer_heights/pallas_call | solution.py:293
  16.8 17.4 %all-to-all-start = ((bf16[64,2,8,128]{3,2,1,0:T(8,128)(2,1)}), bf16[64,2,8,128]{3,2,1,0:T(8,128)(2,1)S(1)}, u32[]{:S(2)}, u32[]{:S(2)}) async-start(bf16[64,2,8,128]{3,2,1,0:T(8,128)(2,1)} %get-tuple-element.21), calls=%async_computation | async-start | bytes 524288 | tf_op jit(solution)/shard_map/all_to_all | solution.py:571
  34.2 2.2 %outer_winds.1 = bf16[4,16,4,8,128]{4,3,2,1,0:T(8,128)(2,1)S(1)} custom-call(s32[1]{0:T(128)} %bitcast.at_ref, f32[3,16,8,1024]{3,2,1,0:T(8,128)S(1)} %get-tuple-element.22.b_ref, f32[3,10,8,1024]{3,2,1,0:T(8,128)S(1)} %get-tuple-element.20.s3_ref), custom_call_target="tpu_custom_call" | custom-call | flops 100000000 | bytes 4000000 | tf_op jit(solution)/shard_map/outer_winds/pallas_call | solution.py:314
  36.5 4.3 %collective-permute-start.8 = (bf16[16,4,8,128]{3,2,1,0:T(8,128)(2,1)S(1)}, bf16[16,4,8,128]{3,2,1,0:T(8,128)(2,1)S(1)}, u32[]{:S(2)}, u32[]{:S(2)}) collective-permute-start(bf16[16,4,8,128]{3,2,1,0:T(8,128)(2,1)S(1)} %get-tuple-element.23), channel_id=1, source_target_pairs={{0,24},{8,16},{16,8},{24,0},{32,56},{40,48},{48,40},{56,32},{64,88... | collective-permute-start | bytes 393224 | tf_op jit(solution)/shard_map/ppermute | solution.py:566
  40.8 2.5 %collective-permute-start.7 = (bf16[16,4,8,128]{3,2,1,0:T(8,128)(2,1)S(1)}, bf16[16,4,8,128]{3,2,1,0:T(8,128)(2,1)S(1)}, u32[]{:S(2)}, u32[]{:S(2)}) collective-permute-start(bf16[16,4,8,128]{3,2,1,0:T(8,128)(2,1)S(1)} %get-tuple-element.24), channel_id=1, source_target_pairs={{0,16},{8,24},{16,0},{24,8},{32,48},{40,56},{48,32},{56,40},{64,80... | collective-permute-start | bytes 393224 | tf_op jit(solution)/shard_map/ppermute | solution.py:566
  43.3 2.2 %collective-permute-start.6 = (bf16[16,4,8,128]{3,2,1,0:T(8,128)(2,1)S(1)}, bf16[16,4,8,128]{3,2,1,0:T(8,128)(2,1)S(1)}, u32[]{:S(2)}, u32[]{:S(2)}) collective-permute-start(bf16[16,4,8,128]{3,2,1,0:T(8,128)(2,1)S(1)} %get-tuple-element.25), channel_id=1, source_target_pairs={{0,8},{8,0},{16,24},{24,16},{32,40},{40,32},{48,56},{56,48},{64,72... | collective-permute-start | bytes 393224 | tf_op jit(solution)/shard_map/ppermute | solution.py:566
  45.5 3.5 %collective-permute-done.7.refs_2_ = bf16[16,4,8,128]{3,2,1,0:T(8,128)(2,1)S(1)} collective-permute-done((bf16[16,4,8,128]{3,2,1,0:T(8,128)(2,1)S(1)}, bf16[16,4,8,128]{3,2,1,0:T(8,128)(2,1)S(1)}, u32[]{:S(2)}, u32[]{:S(2)}) %collective-permute-start.7) | collective-permute-done | bytes 131104 | tf_op jit(solution)/shard_map/ppermute | solution.py:566
  48.9 1.2 %collective-permute-done.6.refs_1_ = bf16[16,4,8,128]{3,2,1,0:T(8,128)(2,1)S(1)} collective-permute-done((bf16[16,4,8,128]{3,2,1,0:T(8,128)(2,1)S(1)}, bf16[16,4,8,128]{3,2,1,0:T(8,128)(2,1)S(1)}, u32[]{:S(2)}, u32[]{:S(2)}) %collective-permute-start.6) | collective-permute-done | bytes 131104 | tf_op jit(solution)/shard_map/ppermute | solution.py:566
  50.2 0.8 ring.1
  51.1 10.9 %all-to-all-start.1 = ((bf16[16,4,4,8,128]{4,3,2,1,0:T(8,128)(2,1)}), bf16[16,4,4,8,128]{4,3,2,1,0:T(8,128)(2,1)S(1)}, u32[]{:S(2)}, u32[]{:S(2)}) async-start(bf16[16,4,4,8,128]{4,3,2,1,0:T(8,128)(2,1)} %ring.1), calls=%async_computation.1 | async-start | bytes 1048576 | tf_op jit(solution)/shard_map/all_to_all | solution.py:578
  63.1 3.4 %collective-permute-start.3 = (bf16[520,128]{1,0:T(8,128)(2,1)S(1)}, bf16[520,128]{1,0:T(8,128)(2,1)S(1)}, u32[]{:S(2)}, u32[]{:S(2)}) collective-permute-start(bf16[520,128]{1,0:T(8,128)(2,1)S(1)} %block.1.own_ref), channel_id=1, source_target_pairs={{0,8},{16,24},{32,40},{48,56},{64,72},{80,88},{96,104},{112,120},{... | collective-permute-start | bytes 399368 | tf_op jit(solution)/shard_map/ppermute | solution.py:548
  66.5 3.9 %collective-permute-start.2 = (bf16[520,128]{1,0:T(8,128)(2,1)S(1)}, bf16[520,128]{1,0:T(8,128)(2,1)S(1)}, u32[]{:S(2)}, u32[]{:S(2)}) collective-permute-start(bf16[520,128]{1,0:T(8,128)(2,1)S(1)} %block.1.own_ref), channel_id=1, source_target_pairs={{8,16},{24,32},{40,48},{56,64},{72,80},{88,96},{104,112},{120,128}... | collective-permute-start | bytes 399368 | tf_op jit(solution)/shard_map/ppermute | solution.py:548
  70.4 20.3 %collective-permute-done.2.west_ref = bf16[520,128]{1,0:T(8,128)(2,1)S(1)} collective-permute-done((bf16[520,128]{1,0:T(8,128)(2,1)S(1)}, bf16[520,128]{1,0:T(8,128)(2,1)S(1)}, u32[]{:S(2)}, u32[]{:S(2)}) %collective-permute-start.2) | collective-permute-done | bytes 133152 | tf_op jit(solution)/shard_map/ppermute | solution.py:548
  90.7 2.7 %collective-permute-start.5 = (bf16[3,520,128]{2,1,0:T(8,128)(2,1)S(1)}, bf16[3,520,128]{2,1,0:T(8,128)(2,1)S(1)}, u32[]{:S(2)}, u32[]{:S(2)}) collective-permute-start(bf16[3,520,128]{2,1,0:T(8,128)(2,1)S(1)} %line.1), channel_id=1, source_target_pairs={{0,1},{2,3},{4,5},{6,7},{1,0},{3,2},{5,4},{7,6},{8,9},{10,11},{12,... | collective-permute-start | bytes 1198088 | tf_op jit(solution)/shard_map/ppermute | solution.py:548
  93.5 3.0 %collective-permute-start.4 = (bf16[3,520,128]{2,1,0:T(8,128)(2,1)S(1)}, bf16[3,520,128]{2,1,0:T(8,128)(2,1)S(1)}, u32[]{:S(2)}, u32[]{:S(2)}) collective-permute-start(bf16[3,520,128]{2,1,0:T(8,128)(2,1)S(1)} %line.1), channel_id=1, source_target_pairs={{1,2},{3,4},{5,6},{2,1},{4,3},{6,5},{9,10},{11,12},{13,14},{10,9},... | collective-permute-start | bytes 1198088 | tf_op jit(solution)/shard_map/ppermute | solution.py:548
  96.5 6.1 %collective-permute-done.4.north_ref = bf16[3,520,128]{2,1,0:T(8,128)(2,1)S(1)} collective-permute-done((bf16[3,520,128]{2,1,0:T(8,128)(2,1)S(1)}, bf16[3,520,128]{2,1,0:T(8,128)(2,1)S(1)}, u32[]{:S(2)}, u32[]{:S(2)}) %collective-permute-start.4) | collective-permute-done | bytes 399392 | tf_op jit(solution)/shard_map/ppermute | solution.py:548
  102.6 5.0 %transform.1.transform_ref = bf16[512,512]{1,0:T(8,128)(2,1)S(1)} custom-call(bf16[520,128]{1,0:T(8,128)(2,1)S(1)} %block.1.own_ref, bf16[520,128]{1,0:T(8,128)(2,1)S(1)} %collective-permute-done.2.west_ref, bf16[520,128]{1,0:T(8,128)(2,1)S(1)} %collective-permute-done.3.east_ref, bf16[3,520,128]{2,1,0:T(8,128)(2,1)S(1)} %collective-permute-done.4.north_ref, ...), custom_call_target="tpu_custom_call" | custom-call | tf_op jit(solution)/shard_map/transform/pallas_call | solution.py:481
  107.7 1.3 %heights.1._ = f32[3,512,256]{2,1,0:T(8,128)} custom-call(bf16[512,512]{1,0:T(8,128)(2,1)S(1)} %transform.1.transform_ref, bf16[64,2,8,128]{3,2,1,0:T(8,128)(2,1)S(1)} %all-to-all-done.h_ref), custom_call_target="tpu_custom_call" | custom-call | flops 134217728 | bytes 1000000 | tf_op jit(solution)/shard_map/heights/pallas_call | solution.py:523
  109.0 1.6 %wind_analysis.1 = f32[3,512,256]{2,1,0:T(8,128)} custom-call(bf16[512,512]{1,0:T(8,128)(2,1)S(1)} %transform.1.transform_ref, bf16[64,4,8,128]{3,2,1,0:T(8,128)(2,1)S(1)} %bitcast.22, f32[3,512,256]{2,1,0:T(8,128)} %heights.1._), custom_call_target="tpu_custom_call", output_to_operand_aliasing={{}: (2, {})} | custom-call | tf_op jit(solution)/shard_map/wind_analysis/pallas_call | solution.py:533
  (19 shorter events, 1.3 us)
Async XLA Ops:
  2.4 9.4 %collective-permute-start = (f32[3,3,8,1024]{3,2,1,0:T(8,128)S(1)}, f32[3,3,8,1024]{3,2,1,0:T(8,128)S(1)}, u32[]{:S(2)}, u32[]{:S(2)}) collective-permute-start(f32[3,3,8,1024]{3,2,1,0:T(8,128)S(1)} %get-tuple-element.16.near_ref), channel_id=1, source_target_pairs={{0,1},{2,3},{4,5},{6,7},{1,0},{3,2},{5,4},{7,6},{8,9},{10,11},{12,... | collective-permute-start | bytes 884744 | tf_op jit(solution)/shard_map/ppermute | solution.py:548
  5.0 8.0 %collective-permute-start.1 = (f32[3,3,8,1024]{3,2,1,0:T(8,128)S(1)}, f32[3,3,8,1024]{3,2,1,0:T(8,128)S(1)}, u32[]{:S(2)}, u32[]{:S(2)}) collective-permute-start(f32[3,3,8,1024]{3,2,1,0:T(8,128)S(1)} %get-tuple-element.17.far_ref), channel_id=1, source_target_pairs={{1,2},{3,4},{5,6},{2,1},{4,3},{6,5},{9,10},{11,12},{13,14},{10,9},... | collective-permute-start | bytes 884744 | tf_op jit(solution)/shard_map/ppermute | solution.py:548
  16.8 34.3 %all-to-all-start = ((bf16[64,2,8,128]{3,2,1,0:T(8,128)(2,1)}), bf16[64,2,8,128]{3,2,1,0:T(8,128)(2,1)S(1)}, u32[]{:S(2)}, u32[]{:S(2)}) async-start(bf16[64,2,8,128]{3,2,1,0:T(8,128)(2,1)} %get-tuple-element.21), calls=%async_computation | async-start | bytes 524288 | tf_op jit(solution)/shard_map/all_to_all | solution.py:571
  36.4 25.6 %copy-start = (s32[1,64,128]{2,1,0:T(8,128)S(1)}, s32[1,64,128]{2,1,0:T(8,128)}, u32[]{:S(2)}) copy-start(s32[1,64,128]{2,1,0:T(8,128)} %param.7) | copy-start | bytes 98308
  36.4 25.6 %copy-start.1 = (f32[1,64,128]{2,1,0:T(8,128)S(1)}, f32[1,64,128]{2,1,0:T(8,128)}, u32[]{:S(2)}) copy-start(f32[1,64,128]{2,1,0:T(8,128)} %param.8) | copy-start | bytes 98308
  36.4 25.6 %copy-start.2 = (f32[1,64,128]{2,1,0:T(8,128)S(1)}, f32[1,64,128]{2,1,0:T(8,128)}, u32[]{:S(2)}) copy-start(f32[1,64,128]{2,1,0:T(8,128)} %param.9) | copy-start | bytes 98308
  36.4 25.6 %copy-start.3 = (s32[1,64]{1,0:T(1,128)S(1)}, s32[1,64]{1,0:T(1,128)}, u32[]{:S(2)}) copy-start(s32[1,64]{1,0:T(1,128)} %count_ref.1) | copy-start | bytes 772
  36.5 9.0 %collective-permute-start.8 = (bf16[16,4,8,128]{3,2,1,0:T(8,128)(2,1)S(1)}, bf16[16,4,8,128]{3,2,1,0:T(8,128)(2,1)S(1)}, u32[]{:S(2)}, u32[]{:S(2)}) collective-permute-start(bf16[16,4,8,128]{3,2,1,0:T(8,128)(2,1)S(1)} %get-tuple-element.23), channel_id=1, source_target_pairs={{0,24},{8,16},{16,8},{24,0},{32,56},{40,48},{48,40},{56,32},{64,88... | collective-permute-start | bytes 393224 | tf_op jit(solution)/shard_map/ppermute | solution.py:566
  40.8 8.2 %collective-permute-start.7 = (bf16[16,4,8,128]{3,2,1,0:T(8,128)(2,1)S(1)}, bf16[16,4,8,128]{3,2,1,0:T(8,128)(2,1)S(1)}, u32[]{:S(2)}, u32[]{:S(2)}) collective-permute-start(bf16[16,4,8,128]{3,2,1,0:T(8,128)(2,1)S(1)} %get-tuple-element.24), channel_id=1, source_target_pairs={{0,16},{8,24},{16,0},{24,8},{32,48},{40,56},{48,32},{56,40},{64,80... | collective-permute-start | bytes 393224 | tf_op jit(solution)/shard_map/ppermute | solution.py:566
  43.3 6.9 %collective-permute-start.6 = (bf16[16,4,8,128]{3,2,1,0:T(8,128)(2,1)S(1)}, bf16[16,4,8,128]{3,2,1,0:T(8,128)(2,1)S(1)}, u32[]{:S(2)}, u32[]{:S(2)}) collective-permute-start(bf16[16,4,8,128]{3,2,1,0:T(8,128)(2,1)S(1)} %get-tuple-element.25), channel_id=1, source_target_pairs={{0,8},{8,0},{16,24},{24,16},{32,40},{40,32},{48,56},{56,48},{64,72... | collective-permute-start | bytes 393224 | tf_op jit(solution)/shard_map/ppermute | solution.py:566
  51.1 57.9 %all-to-all-start.1 = ((bf16[16,4,4,8,128]{4,3,2,1,0:T(8,128)(2,1)}), bf16[16,4,4,8,128]{4,3,2,1,0:T(8,128)(2,1)S(1)}, u32[]{:S(2)}, u32[]{:S(2)}) async-start(bf16[16,4,4,8,128]{4,3,2,1,0:T(8,128)(2,1)} %ring.1), calls=%async_computation.1 | async-start | bytes 1048576 | tf_op jit(solution)/shard_map/all_to_all | solution.py:578
  63.1 7.3 %collective-permute-start.3 = (bf16[520,128]{1,0:T(8,128)(2,1)S(1)}, bf16[520,128]{1,0:T(8,128)(2,1)S(1)}, u32[]{:S(2)}, u32[]{:S(2)}) collective-permute-start(bf16[520,128]{1,0:T(8,128)(2,1)S(1)} %block.1.own_ref), channel_id=1, source_target_pairs={{0,8},{16,24},{32,40},{48,56},{64,72},{80,88},{96,104},{112,120},{... | collective-permute-start | bytes 399368 | tf_op jit(solution)/shard_map/ppermute | solution.py:548
  66.5 24.2 %collective-permute-start.2 = (bf16[520,128]{1,0:T(8,128)(2,1)S(1)}, bf16[520,128]{1,0:T(8,128)(2,1)S(1)}, u32[]{:S(2)}, u32[]{:S(2)}) collective-permute-start(bf16[520,128]{1,0:T(8,128)(2,1)S(1)} %block.1.own_ref), channel_id=1, source_target_pairs={{8,16},{24,32},{40,48},{56,64},{72,80},{88,96},{104,112},{120,128}... | collective-permute-start | bytes 399368 | tf_op jit(solution)/shard_map/ppermute | solution.py:548
  90.7 5.8 %collective-permute-start.5 = (bf16[3,520,128]{2,1,0:T(8,128)(2,1)S(1)}, bf16[3,520,128]{2,1,0:T(8,128)(2,1)S(1)}, u32[]{:S(2)}, u32[]{:S(2)}) collective-permute-start(bf16[3,520,128]{2,1,0:T(8,128)(2,1)S(1)} %line.1), channel_id=1, source_target_pairs={{0,1},{2,3},{4,5},{6,7},{1,0},{3,2},{5,4},{7,6},{8,9},{10,11},{12,... | collective-permute-start | bytes 1198088 | tf_op jit(solution)/shard_map/ppermute | solution.py:548
  93.5 9.2 %collective-permute-start.4 = (bf16[3,520,128]{2,1,0:T(8,128)(2,1)S(1)}, bf16[3,520,128]{2,1,0:T(8,128)(2,1)S(1)}, u32[]{:S(2)}, u32[]{:S(2)}) collective-permute-start(bf16[3,520,128]{2,1,0:T(8,128)(2,1)S(1)} %line.1), channel_id=1, source_target_pairs={{1,2},{3,4},{5,6},{2,1},{4,3},{6,5},{9,10},{11,12},{13,14},{10,9},... | collective-permute-start | bytes 1198088 | tf_op jit(solution)/shard_map/ppermute | solution.py:548

commit v3 on v2

--- a/solution.py
+++ b/solution.py
@@ -489,11 +489,9 @@
 
 
 def analysed_field(transform_ref, slab, f, out_ref, buffer, sems, at):
-    for half in range(2):
-        mean, deviation = centred(slab(half))
-        buffer[f, :, half * LANES : (half + 1) * LANES] = mean + jnp.dot(
-            transform_ref[...], deviation, preferred_element_type=f32
-        )
+    halves = [centred(slab(half)) for half in range(2)]
+    mean, deviation = (jnp.concatenate(part, axis=1) for part in zip(*halves))
+    buffer[f] = mean + jnp.dot(transform_ref[...], deviation, preferred_element_type=f32)
     copy = pltpu.make_async_copy(buffer.at[f], out_ref.at[at], sems.at[f])
     copy.start()
     return copy

time: 111 us -> 111 us (level)
  no operation moved by 1% of the time
where the time goes in v3:
time: 111 us; the launch traced here: 110 us
  starting transfers between devices  55.8 us (50%)
  waiting for transfers between devices  32.5 us (29%)
  Pallas kernels  19.5 us (18%)
  local copies, waits for them, and re-layouts  2.38 us (2%)
    ppermute x6, waiting for transfers between devices, swap(): return lax.ppermute(part, axis, pairs + [(j, i) for i, j in pairs])  27.7 us
    ppermute x6, starting transfers between devices, swap(): return lax.ppermute(part, axis, pairs + [(j, i) for i, j in pairs])  18.6 us
    all_to_all x1, starting transfers between devices, exchange(): return lax.all_to_all(part, 'mem', split_axis=0, concat_axis=0, tiled=True)  17.4 us
    all_to_all x1, starting transfers between devices, per_device(): lax.all_to_all(uv, 'mem', split_axis=0, concat_axis=0, axis_index_groups=...  10.9 us
    ppermute x3, starting transfers between devices, around(): return lax.ppermute(part, 'mem', [(i, i ^ shift) for i in range(size)])  8.98 us
    pallas_call x1, Pallas kernels, make_transform(): pl.pallas_call(transform_kernel, out_shape=jax.ShapeDtypeStruct((n, n), b...  5.01 us
    ppermute x3, waiting for transfers between devices, around(): return lax.ppermute(part, 'mem', [(i, i ^ shift) for i in range(size)])  4.69 us
    pallas_call x1, Pallas kernels, inner_forecast(): pl.pallas_call(inner_kernel, out_shape=(part(rows - 2 * HALO), part(4), p...  3.78 us
  transfers between devices with their start and end apart: 11, of which 6 were waited for; matrix products, arithmetic and copies ran while one was open for 0% of the time, Pallas kernels for 13%

profile of v3, /device:TPU:67, one launch (start us, length us, event | category | flops | bytes accessed | tf_op | source)
XLA Modules:
  0.0 110.4 jit_solution(1764498046717807809)
XLA Ops:
  0.0 2.3 %copy.9 = f32[8,3,16,1024]{3,0,2,1:T(8,128)S(1)} copy(f32[8,3,16,1024]{3,2,1,0:T(8,128)} %param.5) | data formatting | bytes 3145728 | tf_op args[0]
  2.4 2.6 %collective-permute-start = (f32[3,3,8,1024]{3,2,1,0:T(8,128)S(1)}, f32[3,3,8,1024]{3,2,1,0:T(8,128)S(1)}, u32[]{:S(2)}, u32[]{:S(2)}) collective-permute-start(f32[3,3,8,1024]{3,2,1,0:T(8,128)S(1)} %get-tuple-element.16.near_ref), channel_id=1, source_target_pairs={{0,1},{2,3},{4,5},{6,7},{1,0},{3,2},{5,4},{7,6},{8,9},{10,11},{12,... | collective-permute-start | bytes 884744 | tf_op jit(solution)/shard_map/ppermute | solution.py:546
  5.0 3.0 %collective-permute-start.1 = (f32[3,3,8,1024]{3,2,1,0:T(8,128)S(1)}, f32[3,3,8,1024]{3,2,1,0:T(8,128)S(1)}, u32[]{:S(2)}, u32[]{:S(2)}) collective-permute-start(f32[3,3,8,1024]{3,2,1,0:T(8,128)S(1)} %get-tuple-element.17.far_ref), channel_id=1, source_target_pairs={{1,2},{3,4},{5,6},{2,1},{4,3},{6,5},{9,10},{11,12},{13,14},{10,9},... | collective-permute-start | bytes 884744 | tf_op jit(solution)/shard_map/ppermute | solution.py:546
  8.0 3.8 %inner.1 = (f32[3,10,8,1024]{3,2,1,0:T(8,128)S(1)}, f32[3,4,8,1024]{3,2,1,0:T(8,128)S(1)}, f32[3,4,8,1024]{3,2,1,0:T(8,128)S(1)}) custom-call(f32[3,16,8,1024]{3,2,1,0:T(8,128)S(1)} %bitcast.21), custom_call_target="tpu_custom_call" | custom-call | flops 400000000 | bytes 4000000 | tf_op jit(solution)/shard_map/inner/pallas_call | solution.py:141
  11.8 1.2 %collective-permute-done.1.from_far_ref = f32[3,3,8,1024]{3,2,1,0:T(8,128)S(1)} collective-permute-done((f32[3,3,8,1024]{3,2,1,0:T(8,128)S(1)}, f32[3,3,8,1024]{3,2,1,0:T(8,128)S(1)}, u32[]{:S(2)}, u32[]{:S(2)}) %collective-permute-start.1) | collective-permute-done | bytes 294944 | tf_op jit(solution)/shard_map/ppermute | solution.py:546
  13.0 3.7 %outer_heights.1 = (bf16[64,2,8,128]{3,2,1,0:T(8,128)(2,1)}, f32[3,16,8,1024]{3,2,1,0:T(8,128)S(1)}) custom-call(s32[1]{0:T(128)} %bitcast.4.row_ref, f32[3,3,8,1024]{3,2,1,0:T(8,128)S(1)} %get-tuple-element.16.near_ref, f32[3,3,8,1024]{3,2,1,0:T(8,128)S(1)} %get-tuple-element.17.far_ref, f32[3,3,8,1024]{3,2,1,0:T(8,128)S(1)} %collective-permute-done.from_near_ref, ...), custom_call_target="tpu_custom_call" | custom-call | flops 200000000 | bytes 4000000 | tf_op jit(solution)/shard_map/outer_heights/pallas_call | solution.py:293
  16.8 17.4 %all-to-all-start = ((bf16[64,2,8,128]{3,2,1,0:T(8,128)(2,1)}), bf16[64,2,8,128]{3,2,1,0:T(8,128)(2,1)S(1)}, u32[]{:S(2)}, u32[]{:S(2)}) async-start(bf16[64,2,8,128]{3,2,1,0:T(8,128)(2,1)} %get-tuple-element.21), calls=%async_computation | async-start | bytes 524288 | tf_op jit(solution)/shard_map/all_to_all | solution.py:569
  34.2 2.2 %outer_winds.1 = bf16[4,16,4,8,128]{4,3,2,1,0:T(8,128)(2,1)S(1)} custom-call(s32[1]{0:T(128)} %bitcast.at_ref, f32[3,16,8,1024]{3,2,1,0:T(8,128)S(1)} %get-tuple-element.22.b_ref, f32[3,10,8,1024]{3,2,1,0:T(8,128)S(1)} %get-tuple-element.20.s3_ref), custom_call_target="tpu_custom_call" | custom-call | flops 100000000 | bytes 4000000 | tf_op jit(solution)/shard_map/outer_winds/pallas_call | solution.py:314
  36.5 4.3 %collective-permute-start.8 = (bf16[16,4,8,128]{3,2,1,0:T(8,128)(2,1)S(1)}, bf16[16,4,8,128]{3,2,1,0:T(8,128)(2,1)S(1)}, u32[]{:S(2)}, u32[]{:S(2)}) collective-permute-start(bf16[16,4,8,128]{3,2,1,0:T(8,128)(2,1)S(1)} %get-tuple-element.23), channel_id=1, source_target_pairs={{0,24},{8,16},{16,8},{24,0},{32,56},{40,48},{48,40},{56,32},{64,88... | collective-permute-start | bytes 393224 | tf_op jit(solution)/shard_map/ppermute | solution.py:564
  40.8 2.5 %collective-permute-start.7 = (bf16[16,4,8,128]{3,2,1,0:T(8,128)(2,1)S(1)}, bf16[16,4,8,128]{3,2,1,0:T(8,128)(2,1)S(1)}, u32[]{:S(2)}, u32[]{:S(2)}) collective-permute-start(bf16[16,4,8,128]{3,2,1,0:T(8,128)(2,1)S(1)} %get-tuple-element.24), channel_id=1, source_target_pairs={{0,16},{8,24},{16,0},{24,8},{32,48},{40,56},{48,32},{56,40},{64,80... | collective-permute-start | bytes 393224 | tf_op jit(solution)/shard_map/ppermute | solution.py:564
  43.3 2.2 %collective-permute-start.6 = (bf16[16,4,8,128]{3,2,1,0:T(8,128)(2,1)S(1)}, bf16[16,4,8,128]{3,2,1,0:T(8,128)(2,1)S(1)}, u32[]{:S(2)}, u32[]{:S(2)}) collective-permute-start(bf16[16,4,8,128]{3,2,1,0:T(8,128)(2,1)S(1)} %get-tuple-element.25), channel_id=1, source_target_pairs={{0,8},{8,0},{16,24},{24,16},{32,40},{40,32},{48,56},{56,48},{64,72... | collective-permute-start | bytes 393224 | tf_op jit(solution)/shard_map/ppermute | solution.py:564
  45.5 3.5 %collective-permute-done.7.refs_2_ = bf16[16,4,8,128]{3,2,1,0:T(8,128)(2,1)S(1)} collective-permute-done((bf16[16,4,8,128]{3,2,1,0:T(8,128)(2,1)S(1)}, bf16[16,4,8,128]{3,2,1,0:T(8,128)(2,1)S(1)}, u32[]{:S(2)}, u32[]{:S(2)}) %collective-permute-start.7) | collective-permute-done | bytes 131104 | tf_op jit(solution)/shard_map/ppermute | solution.py:564
  48.9 1.2 %collective-permute-done.6.refs_1_ = bf16[16,4,8,128]{3,2,1,0:T(8,128)(2,1)S(1)} collective-permute-done((bf16[16,4,8,128]{3,2,1,0:T(8,128)(2,1)S(1)}, bf16[16,4,8,128]{3,2,1,0:T(8,128)(2,1)S(1)}, u32[]{:S(2)}, u32[]{:S(2)}) %collective-permute-start.6) | collective-permute-done | bytes 131104 | tf_op jit(solution)/shard_map/ppermute | solution.py:564
  50.2 0.8 ring.1
  51.1 10.9 %all-to-all-start.1 = ((bf16[16,4,4,8,128]{4,3,2,1,0:T(8,128)(2,1)}), bf16[16,4,4,8,128]{4,3,2,1,0:T(8,128)(2,1)S(1)}, u32[]{:S(2)}, u32[]{:S(2)}) async-start(bf16[16,4,4,8,128]{4,3,2,1,0:T(8,128)(2,1)} %ring.1), calls=%async_computation.1 | async-start | bytes 1048576 | tf_op jit(solution)/shard_map/all_to_all | solution.py:576
  63.1 3.4 %collective-permute-start.3 = (bf16[520,128]{1,0:T(8,128)(2,1)S(1)}, bf16[520,128]{1,0:T(8,128)(2,1)S(1)}, u32[]{:S(2)}, u32[]{:S(2)}) collective-permute-start(bf16[520,128]{1,0:T(8,128)(2,1)S(1)} %block.1.own_ref), channel_id=1, source_target_pairs={{0,8},{16,24},{32,40},{48,56},{64,72},{80,88},{96,104},{112,120},{... | collective-permute-start | bytes 399368 | tf_op jit(solution)/shard_map/ppermute | solution.py:546
  66.5 3.9 %collective-permute-start.2 = (bf16[520,128]{1,0:T(8,128)(2,1)S(1)}, bf16[520,128]{1,0:T(8,128)(2,1)S(1)}, u32[]{:S(2)}, u32[]{:S(2)}) collective-permute-start(bf16[520,128]{1,0:T(8,128)(2,1)S(1)} %block.1.own_ref), channel_id=1, source_target_pairs={{8,16},{24,32},{40,48},{56,64},{72,80},{88,96},{104,112},{120,128}... | collective-permute-start | bytes 399368 | tf_op jit(solution)/shard_map/ppermute | solution.py:546
  70.4 20.3 %collective-permute-done.2.west_ref = bf16[520,128]{1,0:T(8,128)(2,1)S(1)} collective-permute-done((bf16[520,128]{1,0:T(8,128)(2,1)S(1)}, bf16[520,128]{1,0:T(8,128)(2,1)S(1)}, u32[]{:S(2)}, u32[]{:S(2)}) %collective-permute-start.2) | collective-permute-done | bytes 133152 | tf_op jit(solution)/shard_map/ppermute | solution.py:546
  90.7 2.7 %collective-permute-start.5 = (bf16[3,520,128]{2,1,0:T(8,128)(2,1)S(1)}, bf16[3,520,128]{2,1,0:T(8,128)(2,1)S(1)}, u32[]{:S(2)}, u32[]{:S(2)}) collective-permute-start(bf16[3,520,128]{2,1,0:T(8,128)(2,1)S(1)} %line.1), channel_id=1, source_target_pairs={{0,1},{2,3},{4,5},{6,7},{1,0},{3,2},{5,4},{7,6},{8,9},{10,11},{12,... | collective-permute-start | bytes 1198088 | tf_op jit(solution)/shard_map/ppermute | solution.py:546
  93.5 3.0 %collective-permute-start.4 = (bf16[3,520,128]{2,1,0:T(8,128)(2,1)S(1)}, bf16[3,520,128]{2,1,0:T(8,128)(2,1)S(1)}, u32[]{:S(2)}, u32[]{:S(2)}) collective-permute-start(bf16[3,520,128]{2,1,0:T(8,128)(2,1)S(1)} %line.1), channel_id=1, source_target_pairs={{1,2},{3,4},{5,6},{2,1},{4,3},{6,5},{9,10},{11,12},{13,14},{10,9},... | collective-permute-start | bytes 1198088 | tf_op jit(solution)/shard_map/ppermute | solution.py:546
  96.5 6.1 %collective-permute-done.4.north_ref = bf16[3,520,128]{2,1,0:T(8,128)(2,1)S(1)} collective-permute-done((bf16[3,520,128]{2,1,0:T(8,128)(2,1)S(1)}, bf16[3,520,128]{2,1,0:T(8,128)(2,1)S(1)}, u32[]{:S(2)}, u32[]{:S(2)}) %collective-permute-start.4) | collective-permute-done | bytes 399392 | tf_op jit(solution)/shard_map/ppermute | solution.py:546
  102.6 5.0 %transform.1.transform_ref = bf16[512,512]{1,0:T(8,128)(2,1)S(1)} custom-call(bf16[520,128]{1,0:T(8,128)(2,1)S(1)} %block.1.own_ref, bf16[520,128]{1,0:T(8,128)(2,1)S(1)} %collective-permute-done.2.west_ref, bf16[520,128]{1,0:T(8,128)(2,1)S(1)} %collective-permute-done.3.east_ref, bf16[3,520,128]{2,1,0:T(8,128)(2,1)S(1)} %collective-permute-done.4.north_ref, ...), custom_call_target="tpu_custom_call" | custom-call | tf_op jit(solution)/shard_map/transform/pallas_call | solution.py:481
  107.7 1.2 %heights.1._ = f32[3,512,256]{2,1,0:T(8,128)} custom-call(bf16[512,512]{1,0:T(8,128)(2,1)S(1)} %transform.1.transform_ref, bf16[64,2,8,128]{3,2,1,0:T(8,128)(2,1)S(1)} %all-to-all-done.h_ref), custom_call_target="tpu_custom_call" | custom-call | flops 134217728 | bytes 1000000 | tf_op jit(solution)/shard_map/heights/pallas_call | solution.py:521
  108.9 1.5 %wind_analysis.1 = f32[3,512,256]{2,1,0:T(8,128)} custom-call(bf16[512,512]{1,0:T(8,128)(2,1)S(1)} %transform.1.transform_ref, bf16[64,4,8,128]{3,2,1,0:T(8,128)(2,1)S(1)} %bitcast.22, f32[3,512,256]{2,1,0:T(8,128)} %heights.1._), custom_call_target="tpu_custom_call", output_to_operand_aliasing={{}: (2, {})} | custom-call | tf_op jit(solution)/shard_map/wind_analysis/pallas_call | solution.py:531
  (19 shorter events, 1.3 us)
Async XLA Ops:
  2.4 9.4 %collective-permute-start = (f32[3,3,8,1024]{3,2,1,0:T(8,128)S(1)}, f32[3,3,8,1024]{3,2,1,0:T(8,128)S(1)}, u32[]{:S(2)}, u32[]{:S(2)}) collective-permute-start(f32[3,3,8,1024]{3,2,1,0:T(8,128)S(1)} %get-tuple-element.16.near_ref), channel_id=1, source_target_pairs={{0,1},{2,3},{4,5},{6,7},{1,0},{3,2},{5,4},{7,6},{8,9},{10,11},{12,... | collective-permute-start | bytes 884744 | tf_op jit(solution)/shard_map/ppermute | solution.py:546
  5.0 8.0 %collective-permute-start.1 = (f32[3,3,8,1024]{3,2,1,0:T(8,128)S(1)}, f32[3,3,8,1024]{3,2,1,0:T(8,128)S(1)}, u32[]{:S(2)}, u32[]{:S(2)}) collective-permute-start(f32[3,3,8,1024]{3,2,1,0:T(8,128)S(1)} %get-tuple-element.17.far_ref), channel_id=1, source_target_pairs={{1,2},{3,4},{5,6},{2,1},{4,3},{6,5},{9,10},{11,12},{13,14},{10,9},... | collective-permute-start | bytes 884744 | tf_op jit(solution)/shard_map/ppermute | solution.py:546
  16.8 34.3 %all-to-all-start = ((bf16[64,2,8,128]{3,2,1,0:T(8,128)(2,1)}), bf16[64,2,8,128]{3,2,1,0:T(8,128)(2,1)S(1)}, u32[]{:S(2)}, u32[]{:S(2)}) async-start(bf16[64,2,8,128]{3,2,1,0:T(8,128)(2,1)} %get-tuple-element.21), calls=%async_computation | async-start | bytes 524288 | tf_op jit(solution)/shard_map/all_to_all | solution.py:569
  36.4 25.6 %copy-start = (s32[1,64,128]{2,1,0:T(8,128)S(1)}, s32[1,64,128]{2,1,0:T(8,128)}, u32[]{:S(2)}) copy-start(s32[1,64,128]{2,1,0:T(8,128)} %param.7) | copy-start | bytes 98308
  36.4 25.6 %copy-start.1 = (f32[1,64,128]{2,1,0:T(8,128)S(1)}, f32[1,64,128]{2,1,0:T(8,128)}, u32[]{:S(2)}) copy-start(f32[1,64,128]{2,1,0:T(8,128)} %param.8) | copy-start | bytes 98308
  36.4 25.6 %copy-start.2 = (f32[1,64,128]{2,1,0:T(8,128)S(1)}, f32[1,64,128]{2,1,0:T(8,128)}, u32[]{:S(2)}) copy-start(f32[1,64,128]{2,1,0:T(8,128)} %param.9) | copy-start | bytes 98308
  36.4 25.6 %copy-start.3 = (s32[1,64]{1,0:T(1,128)S(1)}, s32[1,64]{1,0:T(1,128)}, u32[]{:S(2)}) copy-start(s32[1,64]{1,0:T(1,128)} %count_ref.1) | copy-start | bytes 772
  36.5 9.0 %collective-permute-start.8 = (bf16[16,4,8,128]{3,2,1,0:T(8,128)(2,1)S(1)}, bf16[16,4,8,128]{3,2,1,0:T(8,128)(2,1)S(1)}, u32[]{:S(2)}, u32[]{:S(2)}) collective-permute-start(bf16[16,4,8,128]{3,2,1,0:T(8,128)(2,1)S(1)} %get-tuple-element.23), channel_id=1, source_target_pairs={{0,24},{8,16},{16,8},{24,0},{32,56},{40,48},{48,40},{56,32},{64,88... | collective-permute-start | bytes 393224 | tf_op jit(solution)/shard_map/ppermute | solution.py:564
  40.8 8.2 %collective-permute-start.7 = (bf16[16,4,8,128]{3,2,1,0:T(8,128)(2,1)S(1)}, bf16[16,4,8,128]{3,2,1,0:T(8,128)(2,1)S(1)}, u32[]{:S(2)}, u32[]{:S(2)}) collective-permute-start(bf16[16,4,8,128]{3,2,1,0:T(8,128)(2,1)S(1)} %get-tuple-element.24), channel_id=1, source_target_pairs={{0,16},{8,24},{16,0},{24,8},{32,48},{40,56},{48,32},{56,40},{64,80... | collective-permute-start | bytes 393224 | tf_op jit(solution)/shard_map/ppermute | solution.py:564
  43.3 6.9 %collective-permute-start.6 = (bf16[16,4,8,128]{3,2,1,0:T(8,128)(2,1)S(1)}, bf16[16,4,8,128]{3,2,1,0:T(8,128)(2,1)S(1)}, u32[]{:S(2)}, u32[]{:S(2)}) collective-permute-start(bf16[16,4,8,128]{3,2,1,0:T(8,128)(2,1)S(1)} %get-tuple-element.25), channel_id=1, source_target_pairs={{0,8},{8,0},{16,24},{24,16},{32,40},{40,32},{48,56},{56,48},{64,72... | collective-permute-start | bytes 393224 | tf_op jit(solution)/shard_map/ppermute | solution.py:564
  51.1 57.8 %all-to-all-start.1 = ((bf16[16,4,4,8,128]{4,3,2,1,0:T(8,128)(2,1)}), bf16[16,4,4,8,128]{4,3,2,1,0:T(8,128)(2,1)S(1)}, u32[]{:S(2)}, u32[]{:S(2)}) async-start(bf16[16,4,4,8,128]{4,3,2,1,0:T(8,128)(2,1)} %ring.1), calls=%async_computation.1 | async-start | bytes 1048576 | tf_op jit(solution)/shard_map/all_to_all | solution.py:576
  63.1 7.3 %collective-permute-start.3 = (bf16[520,128]{1,0:T(8,128)(2,1)S(1)}, bf16[520,128]{1,0:T(8,128)(2,1)S(1)}, u32[]{:S(2)}, u32[]{:S(2)}) collective-permute-start(bf16[520,128]{1,0:T(8,128)(2,1)S(1)} %block.1.own_ref), channel_id=1, source_target_pairs={{0,8},{16,24},{32,40},{48,56},{64,72},{80,88},{96,104},{112,120},{... | collective-permute-start | bytes 399368 | tf_op jit(solution)/shard_map/ppermute | solution.py:546
  66.5 24.2 %collective-permute-start.2 = (bf16[520,128]{1,0:T(8,128)(2,1)S(1)}, bf16[520,128]{1,0:T(8,128)(2,1)S(1)}, u32[]{:S(2)}, u32[]{:S(2)}) collective-permute-start(bf16[520,128]{1,0:T(8,128)(2,1)S(1)} %block.1.own_ref), channel_id=1, source_target_pairs={{8,16},{24,32},{40,48},{56,64},{72,80},{88,96},{104,112},{120,128}... | collective-permute-start | bytes 399368 | tf_op jit(solution)/shard_map/ppermute | solution.py:546
  90.7 5.8 %collective-permute-start.5 = (bf16[3,520,128]{2,1,0:T(8,128)(2,1)S(1)}, bf16[3,520,128]{2,1,0:T(8,128)(2,1)S(1)}, u32[]{:S(2)}, u32[]{:S(2)}) collective-permute-start(bf16[3,520,128]{2,1,0:T(8,128)(2,1)S(1)} %line.1), channel_id=1, source_target_pairs={{0,1},{2,3},{4,5},{6,7},{1,0},{3,2},{5,4},{7,6},{8,9},{10,11},{12,... | collective-permute-start | bytes 1198088 | tf_op jit(solution)/shard_map/ppermute | solution.py:546
  93.5 9.2 %collective-permute-start.4 = (bf16[3,520,128]{2,1,0:T(8,128)(2,1)S(1)}, bf16[3,520,128]{2,1,0:T(8,128)(2,1)S(1)}, u32[]{:S(2)}, u32[]{:S(2)}) collective-permute-start(bf16[3,520,128]{2,1,0:T(8,128)(2,1)S(1)} %line.1), channel_id=1, source_target_pairs={{1,2},{3,4},{5,6},{2,1},{4,3},{6,5},{9,10},{11,12},{13,14},{10,9},... | collective-permute-start | bytes 1198088 | tf_op jit(solution)/shard_map/ppermute | solution.py:546
